TPU v7x, 256 devices: a whole 4x4x8 slice. The times are simulated.
256 devices in a mesh: ctx: 16 (over z_lo, y), fsdp: 16 (over z_hi, x, core).
Axes of the slice: x: 4, y: 4, z: 8 (z_hi: 2, z_lo: 4; z = z_hi * 4 + z_lo), core: 2. Of those that a mesh axis runs over, the one named last changes fastest.
Arguments:
- inputs: bfloat16 [4096, 7168], P('ctx'), may hold values from -12 to 12
- w_qkv: bfloat16 [7168, 3, 4096], P('ctx', None, 'fsdp'), may hold values from -1 to 1, as said below
- selected: int32 [8, 4], replicated, may hold values from -1 to 7, as said below
- d_attn: bfloat16 [4096, 4096], P('ctx', 'fsdp'), may hold values from -6 to 6
Outputs:
- d_input: bfloat16 [4096, 7168], P('ctx', 'fsdp')
Inputs may be any that keep to these rules, and one draw needn't show every extreme that they name: `selected`: row b lists min(b + 1, 4) different blocks of 0 to b, b among them, in the first slots; the other slots hold -1. `w_qkv`: projection weights scaled by the fan-in.
All inputs are finite; a program needn't handle non-finite values.
Results may differ from a plain program's by a relative error of at most 0.023.
Values may be sent and summed in bfloat16 or wider, within the bound.
A program may use at most 128 MiB of HBM per device.

v0:
```python
import jax
import jax.numpy as jnp
from jax import lax
from jax.sharding import PartitionSpec as P

HD = 128
BLOCK = 512


def stat_rows(stat, row_count, heads):
    return stat[..., 0].transpose(0, 2, 1).reshape(row_count, heads)


def attend_chosen(query, keys_all, values_all, grad_out, selected, first_row):
    row_count, col_count = query.shape
    seq_len = keys_all.shape[0]
    nblocks = seq_len // BLOCK
    heads = col_count // HD
    top_count = selected.shape[1]
    group = min(BLOCK, row_count)
    groups = row_count // group
    scaling = HD ** (-0.5)
    block_ids = jnp.arange(nblocks, dtype=jnp.int32)
    q_block = (first_row + jnp.arange(groups, dtype=jnp.int32) * group) // BLOCK
    picked = q_block[:, None] == block_ids[None, :]
    chosen_ids = jnp.sum(jnp.where(picked[:, :, None], selected[None], 0), axis=1)
    index = jnp.maximum(chosen_ids, 0)
    key_pos = index[:, :, None] * BLOCK + jnp.arange(BLOCK, dtype=jnp.int32)[None, None, :]
    key_pos = key_pos.reshape(groups, top_count * BLOCK)
    slot_valid = jnp.repeat(chosen_ids >= 0, BLOCK, axis=1)
    position_q = (first_row + jnp.arange(row_count, dtype=jnp.int32)).reshape(groups, group)
    allowed = slot_valid[:, None, :] & (position_q[:, :, None] >= key_pos[:, None, :])
    key_heads = keys_all.reshape(nblocks, BLOCK, col_count)[index].reshape(
        groups, top_count * BLOCK, heads, HD
    )
    value_heads = values_all.reshape(nblocks, BLOCK, col_count)[index].reshape(
        groups, top_count * BLOCK, heads, HD
    )
    query_heads = query.reshape(groups, group, heads, HD)
    grad_heads = grad_out.reshape(groups, group, heads, HD)
    scores = (
        jnp.einsum("bqhd,bkhd->bhqk", query_heads, key_heads, preferred_element_type=jnp.float32)
        * scaling
    )
    masked = jnp.where(allowed[:, None], scores, -jnp.inf)
    highest = jnp.max(masked, axis=-1, keepdims=True)
    expo = jnp.exp(masked - highest)
    totals = jnp.sum(expo, axis=-1, keepdims=True)
    probs = expo / totals
    probs_low = probs.astype(jnp.bfloat16)
    attended = jnp.einsum(
        "bhqk,bkhd->bqhd", probs_low, value_heads, preferred_element_type=jnp.float32
    ).astype(jnp.bfloat16)
    delta_rows = jnp.sum(grad_heads.astype(jnp.float32) * attended.astype(jnp.float32), axis=3)
    delta = delta_rows.transpose(0, 2, 1)[..., None]
    dprobs = jnp.einsum(
        "bqhd,bkhd->bhqk", grad_heads, value_heads, preferred_element_type=jnp.float32
    )
    dscores = (probs * (dprobs - delta)).astype(jnp.bfloat16)
    dquery = (
        jnp.einsum("bhqk,bkhd->bqhd", dscores, key_heads, preferred_element_type=jnp.float32)
        * scaling
    )
    dquery = dquery.astype(jnp.bfloat16).reshape(row_count, col_count)
    highest_rows = stat_rows(highest, row_count, heads)
    total_rows = stat_rows(totals, row_count, heads)
    delta_flat = delta_rows.reshape(row_count, heads)
    key_slots = (
        jnp.einsum("bhqk,bqhd->bkhd", dscores, query_heads, preferred_element_type=jnp.float32)
        * scaling
    )
    value_slots = jnp.einsum(
        "bhqk,bqhd->bkhd", probs_low, grad_heads, preferred_element_type=jnp.float32
    )
    onehot = (chosen_ids[:, :, None] == block_ids[None, None, :]).astype(jnp.float32)
    key_term = jnp.einsum(
        "gtn,gtkc->nkc",
        onehot,
        key_slots.reshape(groups, top_count, BLOCK, col_count),
        precision=lax.Precision.HIGHEST,
    ).reshape(seq_len, col_count)
    value_term = jnp.einsum(
        "gtn,gtkc->nkc",
        onehot,
        value_slots.reshape(groups, top_count, BLOCK, col_count),
        precision=lax.Precision.HIGHEST,
    ).reshape(seq_len, col_count)
    return (dquery, key_term, value_term, highest_rows, total_rows, delta_flat)


def shards(inputs, w_qkv, selected, d_attn):
    row_count, width = inputs.shape
    col_count = w_qkv.shape[2]
    first_row = lax.axis_index("ctx") * row_count
    whole_w = lax.all_gather(w_qkv, "ctx", axis=0, tiled=True).reshape(width, 3 * col_count)
    projected = jnp.dot(inputs, whole_w, preferred_element_type=jnp.float32)
    projected = projected.astype(jnp.bfloat16).reshape(row_count, 3, col_count)
    query = projected[:, 0]
    keys_local = projected[:, 1]
    values_local = projected[:, 2]
    keys_all, values_all = (
        lax.all_gather(keys_local, "ctx", axis=0, tiled=True),
        lax.all_gather(values_local, "ctx", axis=0, tiled=True),
    )
    dquery, key_term, value_term, _, _, _ = attend_chosen(
        query, keys_all, values_all, d_attn, selected, first_row
    )
    key_total, value_total = (
        lax.psum_scatter(
            key_term.astype(jnp.bfloat16), "ctx", scatter_dimension=0, tiled=True
        ).astype(jnp.float32),
        lax.psum_scatter(
            value_term.astype(jnp.bfloat16), "ctx", scatter_dimension=0, tiled=True
        ).astype(jnp.float32),
    )
    key_sum = key_total.astype(jnp.bfloat16)
    value_sum = value_total.astype(jnp.bfloat16)
    flat_grads = jnp.stack([dquery, key_sum, value_sum], axis=1).reshape(row_count, 3 * col_count)
    contract = (((1,), (1,)), ((), ()))
    partial_grad = lax.dot_general(
        flat_grads, whole_w, contract, preferred_element_type=jnp.float32
    )
    total = lax.psum_scatter(
        partial_grad.astype(jnp.bfloat16), "fsdp", scatter_dimension=1, tiled=True
    )
    return total


def solution(mesh):
    placed = (P("ctx", None), P("ctx", None, "fsdp"), P(), P("ctx", "fsdp"))
    return jax.shard_map(
        shards, mesh=mesh, in_specs=placed, out_specs=P("ctx", "fsdp"), check_vma=False
    )
```

profile of v0, /device:TPU:97, one launch (start us, length us, event | category | flops | bytes accessed | tf_op | source)
XLA Modules:
  0.0 625.6 jit_solution(6221910780856533034)
XLA Ops:
  6.5 0.0 all-gather.6.cloned.1.call-start
  6.5 0.7 all-gather.6.cloned.1.call-update
  7.3 0.0 all-gather.8.cloned.1.call-start
  7.3 129.5 %all-gather.6.cloned.1.call-done = bf16[7168,3,256]{2,0,1:T(8,128)(2,1)} async-done(((bf16[448,3,256]{2,0,1:T(8,128)(2,1)}), bf16[7168,3,256]{2,0,1:T(8,128)(2,1)}) %all-gather.6.cloned.1.call-update) | async-done | bytes 11010064 | tf_op jit(solution)/shard_map/all_gather | solution.py:95
  136.8 14.8 %copy.15 = bf16[7168,3,256]{0,2,1:T(8,128)(2,1)} copy(bf16[7168,3,256]{2,0,1:T(8,128)(2,1)} %all-gather.6.cloned.1.call-done) | data formatting | bytes 22020096 | tf_op jit(solution)/shard_map/all_gather | solution.py:95
  151.6 0.0 copy-start.8
  151.6 8.3 %convolution_convert_fusion.1 = bf16[256,768]{1,0:T(8,128)(2,1)S(1)} fusion(bf16[256,7168]{1,0:T(8,128)(2,1)} %param.4, bf16[7168,768]{0,1:T(8,128)(2,1)} %bitcast.100), kind=kOutput, calls=%fused_computation.23 | convolution fusion | flops 2818768896 | bytes 15073280 | tf_op jit(solution)/shard_map/dot_general | solution.py:96
  159.9 0.2 copy.16
  160.1 0.7 fusion.39
  160.8 0.0 all-gather.8.cloned.1.call-update
  160.9 0.0 all-gather.10.cloned.1.call-start
  160.9 0.7 all-gather.10.cloned.1.call-update
  161.6 0.2 reduce-scatter.4.cloned.1.call-start
  161.9 0.0 copy-done.8
  161.9 0.1 select_reduce_fusion
  162.0 0.1 broadcast_bitcast_fusion
  162.1 0.0 copy-done.4
  162.1 0.1 copy.23
  162.2 0.1 add.48
  162.3 1.2 compare_and_fusion
  163.6 60.3 %all-gather.8.cloned.1.call-done = bf16[4096,1,256]{0,2,1:T(8,128)(2,1)} async-done(((bf16[256,1,256]{0,2,1:T(8,128)(2,1)}), bf16[4096,1,256]{0,2,1:T(8,128)(2,1)}) %all-gather.8.cloned.1.call-update) | async-done | bytes 2097168 | tf_op jit(solution)/shard_map/all_gather | solution.py:102
  223.9 3.3 copy.17
  227.1 0.6 gather_fusion
  227.8 0.3 reshape.318
  228.1 0.8 copy.26
  228.9 70.2 %all-gather.10.cloned.1.call-done = bf16[4096,1,256]{0,2,1:T(8,128)(2,1)} async-done(((bf16[256,1,256]{0,2,1:T(8,128)(2,1)}), bf16[4096,1,256]{0,2,1:T(8,128)(2,1)}) %all-gather.10.cloned.1.call-update) | async-done | bytes 2097168 | tf_op jit(solution)/shard_map/all_gather | solution.py:103
  299.1 3.3 copy.20
  302.4 1.6 gather_fusion.1
  304.0 1.4 reshape.321
  305.4 2.1 copy.24
  307.4 0.0 copy-done.5
  307.4 0.0 copy-done.6
  307.4 3.7 fusion.40
  311.1 2.9 fusion.13
  314.1 0.0 copy-done.2
  314.1 0.8 fusion.19
  314.9 0.0 copy-done.3
  314.9 0.0 copy-start.7
  314.9 0.7 fusion.2
  315.7 0.0 copy-start
  315.7 1.4 copy-done
  317.0 0.0 copy-done.7
  317.0 1.8 fusion.4
  318.8 3.6 reshape.323
  322.5 4.1 copy.27
  326.6 4.1 convolution_convert_fusion
  330.7 1.7 copy.28
  332.4 0.0 reduce-scatter.4.cloned.1.call-update
  332.4 0.3 reduce-scatter.6.cloned.1.call-start
  332.7 0.9 convolution_bitcast_fusion.1
  333.6 8.6 %copy.31 = f32[1,2048,2,128]{3,2,1,0:T(2,128)} copy(f32[1,2048,2,128]{3,1,2,0:T(8,128)S(1)} %convolution_bitcast_fusion.1) | data formatting | bytes 4194304 | tf_op jit(solution)/shard_map/bhqk,bqhd->bkhd/transpose | solution.py:72
  342.2 2.9 reshape.324
  345.1 3.4 fusion.10
  348.5 1.7 copy.33
  350.3 0.0 reduce-scatter.6.cloned.1.call-update
  350.3 0.0 reduce-scatter.8.cloned.1.call-start
  350.3 1.5 copy-done.1
  351.8 0.8 fusion.14
  352.7 0.1 copy.34
  352.8 60.4 %reduce-scatter.4.cloned.1.call-done = bf16[256,256]{1,0:T(8,128)(2,1)} async-done(((bf16[4096,256]{1,0:T(8,128)(2,1)}), bf16[256,256]{1,0:T(8,128)(2,1)}) %reduce-scatter.4.cloned.1.call-update) | async-done | bytes 131088 | tf_op jit(solution)/shard_map/reduce_scatter | solution.py:109
  413.2 86.2 %reduce-scatter.6.cloned.1.call-done = bf16[256,256]{1,0:T(8,128)(2,1)} async-done(((bf16[4096,256]{1,0:T(8,128)(2,1)}), bf16[256,256]{1,0:T(8,128)(2,1)}) %reduce-scatter.6.cloned.1.call-update) | async-done | bytes 131088 | tf_op jit(solution)/shard_map/reduce_scatter | solution.py:112
  499.3 9.3 %fusion.1 = bf16[256,7168]{0,1:T(8,128)(2,1)} fusion(bf16[7168,3,256]{2,0,1:T(8,128)(2,1)} %all-gather.6.cloned.1.call-done, bf16[256,1,256]{2,0,1:T(8,128)(2,1)} %bitcast.115, bf16[256,1,256]{2,0,1:T(8,128)(2,1)} %bitcast.114, bf16[256,1,256]{2,0,1:T(8,128)(2,1)S(1)} %copy.34), kind=kOutput, calls=%fused_computation.4 | convolution fusion | flops 2820800512 | bytes 15073280 | tf_op jit(solution)/shard_map/dot_general | solution.py:120
  508.6 0.0 reduce-scatter.8.cloned.1.call-update
  508.6 110.1 %reduce-scatter.8.cloned.1.call-done = bf16[256,448]{0,1:T(8,128)(2,1)} async-done(((bf16[256,7168]{0,1:T(8,128)(2,1)}), bf16[256,448]{0,1:T(8,128)(2,1)}) %reduce-scatter.8.cloned.1.call-update) | async-done | bytes 229392 | tf_op jit(solution)/shard_map/reduce_scatter | solution.py:123
  (15 shorter events, 0.1 us)
Async XLA Ops:
  6.5 130.3 %all-gather.6.cloned.1.call-start = ((), (), s32[]{:S(2)}) async-start(), calls=%async_computation.3 | async-start | bytes 11698176 | tf_op jit(solution)/shard_map/all_gather | solution.py:95
  7.3 216.6 %all-gather.8.cloned.1.call-start = ((), (), s32[]{:S(2)}) async-start(), calls=%async_computation.7 | async-start | bytes 2228224 | tf_op jit(solution)/shard_map/all_gather | solution.py:102
  151.6 10.3 %copy-start.8 = (s32[8,4]{0,1:T(4,128)S(1)}, s32[8,4]{0,1:T(4,128)}, u32[]{:S(2)}) copy-start(s32[8,4]{0,1:T(4,128)} %param.6) | copy-start | bytes 388
  151.6 10.5 %copy-start.4 = (bf16[256,256]{1,0:T(8,128)(2,1)S(1)}, bf16[256,256]{1,0:T(8,128)(2,1)}, u32[]{:S(2)}) copy-start(bf16[256,256]{1,0:T(8,128)(2,1)} %param.7) | copy-start | bytes 393220
  160.9 138.2 %all-gather.10.cloned.1.call-start = ((), (), s32[]{:S(2)}) async-start(), calls=%async_computation.8 | async-start | bytes 2228224 | tf_op jit(solution)/shard_map/all_gather | solution.py:103
  161.6 251.6 %reduce-scatter.4.cloned.1.call-start = ((), (), s32[]{:S(2)}) async-start(), calls=%async_computation.4 | async-start | bytes 2228224 | tf_op jit(solution)/shard_map/reduce_scatter | solution.py:109
  304.0 3.5 copy-start.5
  304.0 3.5 copy-start.6
  311.1 3.0 copy-start.2
  311.1 3.8 copy-start.3
  314.9 2.1 copy-start.7
  315.7 1.4 copy-start
  332.4 166.9 %reduce-scatter.6.cloned.1.call-start = ((), (), s32[]{:S(2)}) async-start(), calls=%async_computation.5 | async-start | bytes 2228224 | tf_op jit(solution)/shard_map/reduce_scatter | solution.py:112
  350.3 1.6 copy-start.1
  350.3 268.5 %reduce-scatter.8.cloned.1.call-start = ((), (), s32[]{:S(2)}) async-start(), calls=%async_computation.6 | async-start | bytes 3899392 | tf_op jit(solution)/shard_map/reduce_scatter | solution.py:123
Sparse Core Ops, SparseCore 0:
  9.1 127.6 all-gather.5
  161.0 62.8 all-gather.7
  225.6 73.4 all-gather.9
  332.6 80.5 reduce-scatter.3
  415.5 83.7 reduce-scatter.5
  508.7 109.9 reduce-scatter.7
where the time goes:
time: 631 us; the launch traced here: 626 us
  waiting for transfers between devices  518 us (82%)
  local copies, waits for them, and re-layouts  55 us (9%)
  matrix products  33.8 us (5%)
  between operations  13.7 us (2%)
    all_gather x1, waiting for transfers between devices, shards(): lax.all_gather(w_qkv, 'ctx', axis=0, tiled=True)  130 us
    reduce_scatter x1, waiting for transfers between devices, shards(): lax.psum_scatter(partial_grad.astype(jnp.bfloat16), 'fsdp', scatter_dimen...  110 us
    reduce_scatter x1, waiting for transfers between devices, shards(): lax.psum_scatter(value_term.astype(jnp.bfloat16), 'ctx', scatter_dimensio...  86.2 us
    all_gather x1, waiting for transfers between devices, shards(): lax.all_gather(values_local, 'ctx', axis=0, tiled=True)  70.2 us
    reduce_scatter x1, waiting for transfers between devices, shards(): lax.psum_scatter(key_term.astype(jnp.bfloat16), 'ctx', scatter_dimension=...  60.4 us
    all_gather x1, waiting for transfers between devices, shards(): lax.all_gather(keys_local, 'ctx', axis=0, tiled=True)  60.3 us
    another operation x7, local copies, waits for them, and re-layouts  15.3 us
    all_gather x1, local copies, waits for them, and re-layouts, shards(): lax.all_gather(w_qkv, 'ctx', axis=0, tiled=True)  14.8 us
  transfers between devices with their start and end apart: 6, of which 6 were waited for; matrix products, arithmetic and copies ran while one was open for 4% of the time, Pallas kernels for 0%

commit v1 on v0

v1 whole, which is shorter than its diff:
```python
import functools

import jax
import jax.numpy as jnp
from jax import lax
from jax.experimental import pallas as pl
from jax.experimental.pallas import tpu as pltpu
from jax.sharding import PartitionSpec as P

MESH = pl.DeviceIdType.MESH
F32 = jnp.float32
BF16 = jnp.bfloat16
HD = 128
BLOCK = 512
TOP = 4
SCALE = HD ** (-0.5)
VMEM_BYTES = 60 * 1024 * 1024


def place():
    c = lax.axis_index("ctx")
    f = lax.axis_index("fsdp")
    return (
        lax.div(c, 4), lax.rem(c, 4),
        lax.div(f, 8), lax.rem(lax.div(f, 2), 4), lax.rem(f, 2),
    )


def device(z, y, zh, x, k):
    return (z * 4 + y, zh * 8 + x * 2 + k)


def turn(i, by):
    return lax.rem(i + by, 4)


def rows(start, size):
    return pl.ds(pl.multiple_of(start, size & -size), size)


class Mail:
    def __init__(self, send_sems):
        self.send_sems = send_sems
        self.used = 0
        self.sent = []

    def copy(self, src, dst, recv, dev):
        sem = self.send_sems.at[self.used]
        self.used += 1
        return pltpu.make_async_remote_copy(
            src_ref=src, dst_ref=dst, send_sem=sem, recv_sem=recv,
            device_id=dev, device_id_type=MESH,
        )

    def send(self, src, dst, recv, dev):
        copy = self.copy(src, dst, recv, dev)
        copy.start()
        self.sent.append((copy, None, None))

    def send_or_keep(self, away, src, dst, recv, dev):
        copy = self.copy(src, dst, recv, dev)
        stay = pltpu.make_async_copy(src, dst, recv)

        @pl.when(away)
        def _():
            copy.start()

        @pl.when(jnp.logical_not(away))
        def _():
            stay.start()

        self.sent.append((copy, away, None))

    def send_if(self, away, src, dst, recv, dev):
        copy = self.copy(src, dst, recv, dev)

        @pl.when(away)
        def _():
            copy.start()

        self.sent.append((copy, away, None))

    def flush(self):
        for copy, away, _ in self.sent:
            if away is None:
                copy.wait_send()
            else:
                pl.when(away)(copy.wait_send)


def got(dst, recv):
    pltpu.make_async_copy(dst, dst, recv).wait()


class Ring:
    def __init__(self, mail, view, pos, core, right, left, partner, ring, cores):
        self.mail, self.view, self.pos, self.core = mail, view, pos, core
        self.right, self.left, self.partner = right, left, partner
        self.ring, self.cores = ring, cores

    def pass_on(self, pos, half, recv, dev):
        ref = self.view(self.core, pos, half)
        self.mail.send(ref, ref, recv, dev)

    def start(self):
        self.pass_on(self.pos, None, self.ring.at[0], self.right)
        self.pass_on(self.pos, None, self.ring.at[1], self.left)
        self.pass_on(self.pos, None, self.cores.at[0], self.partner)

    def relay(self):
        before, after = turn(self.pos, 3), turn(self.pos, 1)
        got(self.view(self.core, before, None), self.ring.at[0])
        self.pass_on(before, 0, self.ring.at[2], self.right)
        self.pass_on(before, None, self.cores.at[1], self.partner)
        got(self.view(self.core, after, None), self.ring.at[1])
        self.pass_on(after, 1, self.ring.at[3], self.left)
        self.pass_on(after, None, self.cores.at[2], self.partner)

    def finish(self):
        far = turn(self.pos, 2)
        for half in (0, 1):
            got(self.view(self.core, far, half), self.ring.at[2 + half])
            self.pass_on(far, half, self.cores.at[3 + half], self.partner)

    def settle(self):
        other = 1 - self.core
        before, after, far = turn(self.pos, 3), turn(self.pos, 1), turn(self.pos, 2)
        got(self.view(other, self.pos, None), self.cores.at[0])
        got(self.view(other, before, None), self.cores.at[1])
        got(self.view(other, after, None), self.cores.at[2])
        got(self.view(other, far, 0), self.cores.at[3])
        got(self.view(other, far, 1), self.cores.at[4])


def enter(devices, more=0):
    barrier = pltpu.get_barrier_semaphore()
    for dev in devices:
        pl.semaphore_signal(barrier, inc=1, device_id=dev, device_id_type=MESH)
    return barrier, len(devices) + more


def project_kernel(
    inp, w3, d_attn, q_out, kv_out, do_out, w_out,
    wall, xall, dall, part, parts_in, own, kvall,
    send_sems, load_sems, w_ring, w_cores, x_z, x_x, d_sems, p_sems, kv_ring, kv_cores, out_sems,
):
    z, y, zh, x, j = place()
    here = functools.partial(device, z, y, zh, x)
    partner = here(1 - j)
    right = device(z, turn(y, 1), zh, x, j)
    left = device(z, turn(y, 3), zh, x, j)
    d = wall.shape[1] // 4
    dq = wall.shape[1]

    loads = []
    for s in (0, 1):
        for at, p in ((0, 1), (1, 2), (2, 0)):
            loads.append(pltpu.make_async_copy(
                w3.at[p, :, pl.ds(HD * s, HD)],
                wall.at[2 * j + s, rows(d * y, d), pl.ds(HD * at, HD)],
                load_sems.at[3 * s + at],
            ))
    own_x = pltpu.make_async_copy(
        inp.at[rows(HD * j, HD), rows(dq * z, dq)], xall.at[rows(HD * z, HD)], load_sems.at[6]
    )
    for copy in loads:
        copy.start()
    own_x.start()

    peers = [device(turn(z, t), y, zh, x, k) for t in (1, 2, 3) for k in (j, 1 - j)]
    peers += [partner, right, left]
    peers += [device(z, y, zh, turn(x, u), j) for u in (1, 2, 3)]
    barrier, expected = enter(peers)
    pl.semaphore_wait(barrier, expected)

    mail = Mail(send_sems)

    def w_view(s):
        def view(core, pos, half):
            if half is None:
                return wall.at[2 * core + s, rows(d * pos, d)]
            return wall.at[2 * core + s, rows(d * pos + (d // 2) * half, d // 2)]
        return view

    w_rings = [
        Ring(mail, w_view(s), y, j, right, left, partner, w_ring.at[s], w_cores.at[s])
        for s in (0, 1)
    ]
    for copy in loads[:3]:
        copy.wait()
    w_rings[0].start()

    piece = HD // 4
    for t in (1, 2, 3):
        zd = turn(z, t)
        mail.send(
            inp.at[rows(HD * j + piece * x, piece), rows(dq * zd, dq)],
            xall.at[rows(HD * z + piece * x, piece)],
            x_z.at[t - 1], device(zd, y, zh, x, j),
        )
    for copy in loads[3:]:
        copy.wait()
    for t in (1, 2, 3):
        zs = turn(z, 4 - t)
        mine = xall.at[rows(HD * zs + piece * x, piece)]
        got(mine, x_z.at[t - 1])
        for u in (1, 3, 2):
            mail.send(mine, mine, x_x.at[t - 1, u - 1], device(z, y, zh, turn(x, u), j))
    w_rings[0].relay()
    w_rings[1].start()
    for s in (0, 1):
        for k in (0, 1):
            zd = 2 * j + s
            away = jnp.logical_or(zd != z, j != k)
            mail.send_or_keep(
                away,
                d_attn.at[pl.ds(HD * k, HD), pl.ds(HD * s, HD)],
                dall.at[z], d_sems.at[z], device(zd, y, zh, x, k),
            )
    own_x.wait()
    for t in (1, 2, 3):
        zs = turn(z, 4 - t)
        for u in (1, 3, 2):
            xs = turn(x, 4 - u)
            got(xall.at[rows(HD * zs + piece * xs, piece)], x_x.at[t - 1, u - 1])
    w_rings[0].finish()
    w_rings[0].settle()

    def project(s, turned):
        head = 2 * lax.rem(j + turned, 2) + s
        slot = 2 * s + turned
        away = head != z

        for tile in (0, 1):
            at = pl.ds(256 * tile, 256)
            total = jnp.dot(xall[at], wall[head], preferred_element_type=F32)
            part[slot, at] = total.astype(BF16)

            @pl.when(jnp.logical_not(away))
            def _():
                own[at] = total

        mail.send_if(
            away, part.at[slot], parts_in.at[z], p_sems.at[z], device(head, y, zh, x, j)
        )

    project(0, 0)
    project(0, 1)
    w_rings[1].relay()
    w_rings[1].finish()
    w_rings[1].settle()
    project(1, 0)
    project(1, 1)
    keep_w = pltpu.make_async_copy(wall, w_out, out_sems.at[0])
    keep_w.start()

    for t in (1, 2, 3):
        zs = turn(z, t)
        got(parts_in.at[zs], p_sems.at[zs])
    for run in range(4):
        at = pl.ds(HD * run, HD)
        total = own[at]
        for t in (1, 2, 3):
            total += parts_in[turn(z, t), at].astype(F32)
        low = total.astype(BF16)
        kvall[run, y, j] = low[:, : 2 * HD]
        q_out[at] = low[:, 2 * HD :]

    def kv_view(core, pos, half):
        if half is None:
            return kvall.at[:, pos, core]
        return kvall.at[pl.ds(2 * half, 2), pos, core]

    kv = Ring(mail, kv_view, y, j, right, left, partner, kv_ring, kv_cores)
    kv.start()
    for zs in range(4):
        got(dall.at[zs], d_sems.at[zs])
    do_out[...] = dall[...]
    kv.relay()
    kv.finish()
    kv.settle()
    keep_kv = pltpu.make_async_copy(kvall, kv_out, out_sems.at[1])
    keep_kv.start()
    mail.flush()
    keep_w.wait()
    keep_kv.wait()


def project_and_gather(inputs, w3, d_attn):
    rows_here, width = inputs.shape
    quarter = width // 4
    any_space = pl.BlockSpec(memory_space=pl.ANY)
    vmem = pl.BlockSpec(memory_space=pltpu.VMEM)
    dma = pltpu.SemaphoreType.DMA
    return pl.pallas_call(
        project_kernel,
        name="project_and_gather",
        out_shape=(
            jax.ShapeDtypeStruct((4 * HD, HD), BF16),
            jax.ShapeDtypeStruct((4, 4, 2, HD, 2 * HD), BF16),
            jax.ShapeDtypeStruct((4, HD, HD), BF16),
            jax.ShapeDtypeStruct((4, quarter, 3 * HD), BF16),
        ),
        in_specs=[any_space] * 3,
        out_specs=(vmem, any_space, vmem, any_space),
        scratch_shapes=[
            pltpu.VMEM((4, quarter, 3 * HD), BF16),
            pltpu.VMEM((4 * HD, quarter), BF16),
            pltpu.VMEM((4, HD, HD), BF16),
            pltpu.VMEM((4, 4 * HD, 3 * HD), BF16),
            pltpu.VMEM((4, 4 * HD, 3 * HD), BF16),
            pltpu.VMEM((4 * HD, 3 * HD), F32),
            pltpu.VMEM((4, 4, 2, HD, 2 * HD), BF16),
            dma((60,)), dma((7,)), dma((2, 4)), dma((2, 5)), dma((3,)), dma((3, 3)),
            dma((4,)), dma((4,)), dma((4,)), dma((5,)), dma((2,)),
        ],
        compiler_params=pltpu.CompilerParams(
            collective_id=0, has_side_effects=True, vmem_limit_bytes=VMEM_BYTES
        ),
    )(inputs, w3, d_attn)


def attend_kernel(selected, q_ref, kv_ref, do_ref, dq_ref, dkv_ref, score, soft, total):
    _, y, _, _, j = place()
    total[...] = jnp.zeros_like(total)
    contract = lambda a, b: (((a,), (b,)), ((), ()))
    dot = functools.partial(lax.dot_general, preferred_element_type=F32)
    key_at = lax.broadcasted_iota(jnp.int32, (BLOCK, HD), 0)
    query_at = lax.broadcasted_iota(jnp.int32, (BLOCK, HD), 1)

    def tile(run, carry):
        first = (run * 4 + y) * 256 + HD * j
        block = lax.div(first, BLOCK)
        q = q_ref[run]
        do = do_ref[run]
        highest = jnp.full((1, HD), -jnp.inf, F32)
        for t in range(TOP):
            chosen = selected[block, t]
            kb = jnp.maximum(chosen, 0)
            s = dot(kv_ref[kb, :, :HD], q, contract(1, 1)) * SCALE
            limit = jnp.where(chosen >= 0, first - kb * BLOCK, -2 * BLOCK)
            s = jnp.where(key_at - query_at <= limit, s, -jnp.inf)
            score[t] = s
            highest = jnp.maximum(highest, jnp.max(s, axis=0, keepdims=True))
        totals = jnp.zeros((1, HD), F32)
        for t in range(TOP):
            e = jnp.exp(score[t] - highest)
            score[t] = e
            totals += jnp.sum(e, axis=0, keepdims=True)
        share = 1.0 / totals
        attended = jnp.zeros((HD, HD), F32)
        for t in range(TOP):
            kb = jnp.maximum(selected[block, t], 0)
            p = score[t] * share
            low = p.astype(BF16)
            score[t] = p
            soft[t] = low
            attended += dot(kv_ref[kb, :, HD:], low, contract(0, 0))
        attended = attended.astype(BF16).astype(F32)
        delta = jnp.sum(do.astype(F32).T * attended, axis=0, keepdims=True)
        dq = jnp.zeros((HD, HD), F32)
        for t in range(TOP):
            kb = jnp.maximum(selected[block, t], 0)
            dp = dot(kv_ref[kb, :, HD:], do, contract(1, 1))
            ds = (score[t] * (dp - delta)).astype(BF16)
            total[kb, :, :HD] += dot(ds, q, contract(1, 0))
            total[kb, :, HD:] += dot(soft[t], do, contract(1, 0))
            dq += dot(ds, kv_ref[kb, :, :HD], contract(0, 0))
        dq_ref[run] = (dq * SCALE).astype(BF16)
        return carry

    lax.fori_loop(0, 4, tile, 0)
    for b in range(8):
        dkv_ref[b, :, :HD] = (total[b, :, :HD] * SCALE).astype(BF16)
        dkv_ref[b, :, HD:] = total[b, :, HD:].astype(BF16)


def attend(selected, q, kv, do):
    vmem = pl.BlockSpec(memory_space=pltpu.VMEM)
    return pl.pallas_call(
        attend_kernel,
        name="attend",
        out_shape=(
            jax.ShapeDtypeStruct((4, HD, HD), BF16),
            jax.ShapeDtypeStruct((8, BLOCK, 2 * HD), BF16),
        ),
        in_specs=[pl.BlockSpec(memory_space=pltpu.SMEM), vmem, vmem, vmem],
        out_specs=(vmem, vmem),
        scratch_shapes=[
            pltpu.VMEM((TOP, BLOCK, HD), F32),
            pltpu.VMEM((TOP, BLOCK, HD), BF16),
            pltpu.VMEM((8, BLOCK, 2 * HD), F32),
        ],
        compiler_params=pltpu.CompilerParams(vmem_limit_bytes=VMEM_BYTES),
    )(selected, q, kv, do)


def owner_x(z, pair, zp):
    same = 2 * lax.rem(z, 2) + pair
    other = 2 * (1 - lax.rem(z, 2)) + 1 - pair
    return jnp.where(zp == 0, same, other)


def portion(z, x):
    same = lax.div(x, 2) == lax.rem(z, 2)
    pair = jnp.where(same, lax.rem(x, 2), 1 - lax.rem(x, 2))
    return pair, jnp.where(same, 0, 1)


def gradient_kernel(
    dkv, dq, w_in, out,
    wall, gall, core_out, core_in, near_out, far_out, far_in, near_in, own_kv,
    x_out, x_in, own_x, fin, fin_in,
    send_sems, load_sem, core_sems, far_sems, near_sems, q_sems, g_sems, xf_sems, xn_sems, f_sems,
):
    z, y, zh, x, j = place()
    d = wall.shape[1] // 4
    partner = device(z, y, zh, x, 1 - j)
    right = device(z, turn(y, 1), zh, x, j)
    left = device(z, turn(y, 3), zh, x, j)
    x_right = device(z, y, zh, turn(x, 1), j)
    x_left = device(z, y, zh, turn(x, 3), j)
    across = [device(turn(z, t), y, zh, x, j) for t in (1, 2, 3)]
    f = lax.axis_index("fsdp")
    source_z = lax.div(f, 4)
    source_x = owner_x(source_z, lax.div(lax.rem(f, 4), 2), lax.div(z, 2))

    load = pltpu.make_async_copy(w_in, wall, load_sem)
    load.start()

    barrier, expected = enter([partner, right, left, x_right, x_left] + across, more=4)
    for h in (0, 1):
        for k in (0, 1):
            pl.semaphore_signal(
                barrier, inc=1, device_id=device(source_z, y, h, source_x, k),
                device_id_type=MESH,
            )
    pl.semaphore_wait(barrier, expected)

    mail = Mail(send_sems)
    for n, t in enumerate((2, 1, 3, 0)):
        yd = turn(y, t)
        mail.send(dkv.at[:, yd, 1 - j], core_in.at[n], core_sems.at[n], partner)
    for t in (1, 2, 3):
        mail.send(dq, gall.at[z, :, pl.ds(2 * HD, HD)], q_sems.at[z], across[t - 1])
    gall[z, :, pl.ds(2 * HD, HD)] = dq[...]

    def chip_sum(n, t, half):
        at = pl.ds(2 * half, 2)
        yd = turn(y, t)
        return dkv[at, yd, j].astype(F32) + core_in[n, at].astype(F32)

    got(core_in.at[0], core_sems.at[0])
    for half, dev in ((0, right), (1, left)):
        far_out[half] = chip_sum(0, 2, half).astype(BF16)
        mail.send(far_out.at[half], far_in.at[half], far_sems.at[half], dev)
    for side, (t, dev) in enumerate(((1, right), (3, left))):
        got(core_in.at[1 + side], core_sems.at[1 + side])
        alone = 1 - side
        near_out[side, alone] = chip_sum(1 + side, t, alone).astype(BF16)
        mail.send(
            near_out.at[side, alone], near_in.at[side, alone], near_sems.at[side, alone], dev
        )
    for side, (t, dev) in enumerate(((1, right), (3, left))):
        got(far_in.at[side], far_sems.at[side])
        near_out[side, side] = (
            chip_sum(1 + side, t, side) + far_in[side].astype(F32)
        ).astype(BF16)
        mail.send(
            near_out.at[side, side], near_in.at[side, side], near_sems.at[side, side], dev
        )
    got(core_in.at[3], core_sems.at[3])
    for half in (0, 1):
        own_kv[half] = chip_sum(3, 0, half)
    for side in (0, 1):
        for half in (1 - side, side):
            got(near_in.at[side, half], near_sems.at[side, half])
    for half in (0, 1):
        for i in (0, 1):
            total = own_kv[half, i]
            for side in (0, 1):
                total += near_in[side, half, i].astype(F32)
            gall[z, pl.ds(HD * (2 * half + i), HD), pl.ds(0, 2 * HD)] = total.astype(BF16)
    mine = gall.at[z, :, pl.ds(0, 2 * HD)]
    for t in (1, 2, 3):
        mail.send(mine, mine, g_sems.at[z], across[t - 1])
    load.wait()
    for t in (1, 2, 3):
        zs = turn(z, t)
        got(gall.at[zs, :, pl.ds(2 * HD, HD)], q_sems.at[zs])
        got(gall.at[zs, :, pl.ds(0, 2 * HD)], g_sems.at[zs])

    def part(t, e):
        pair, zp = portion(z, turn(x, t))
        at = rows(256 * zp, 256)
        cols = rows(d * (2 * pair + e), d)
        total = jnp.zeros((256, d), F32)
        for h in range(4):
            total += lax.dot_general(
                gall[h, at], wall[h, cols], (((1,), (1,)), ((), ())),
                preferred_element_type=F32,
            )
        return total

    for half, dev in ((0, x_right), (1, x_left)):
        x_out[half] = part(2, half).astype(BF16)
        mail.send(x_out.at[half], x_in.at[half], xf_sems.at[half], dev)
    for side, (t, dev) in enumerate(((1, x_right), (3, x_left))):
        alone = 1 - side
        x_out[2 + side] = part(t, alone).astype(BF16)
        mail.send(x_out.at[2 + side], x_in.at[2 + side], xn_sems.at[side], dev)
    for side, (t, dev) in enumerate(((1, x_right), (3, x_left))):
        total = part(t, side)
        got(x_in.at[side], xf_sems.at[side])
        x_out[4 + side] = (total + x_in[side].astype(F32)).astype(BF16)
        mail.send(x_out.at[4 + side], x_in.at[4 + side], xn_sems.at[2 + side], dev)
    for e in (0, 1):
        own_x[e] = part(0, e)
    for side in (0, 1):
        got(x_in.at[2 + side], xn_sems.at[side])
        got(x_in.at[4 + side], xn_sems.at[2 + side])
    pair, zp = portion(z, x)
    for e in (0, 1):
        fin[e] = (
            own_x[e] + x_in[2 + 1 - e].astype(F32) + x_in[4 + e].astype(F32)
        ).astype(BF16)
        for i in (0, 1):
            run = 2 * zp + i
            fd = 4 * z + 2 * pair + e
            away = jnp.logical_or(run != z, fd != f)
            mail.send_or_keep(
                away, fin.at[e, pl.ds(HD * i, HD)], fin_in.at[zh, j], f_sems.at[zh, j],
                (run * 4 + y, fd),
            )
    for h in (0, 1):
        for k in (0, 1):
            got(fin_in.at[h, k], f_sems.at[h, k])
    for k in (0, 1):
        out[pl.ds(HD * k, HD)] = (
            fin_in[0, k].astype(F32) + fin_in[1, k].astype(F32)
        ).astype(BF16)
    mail.flush()


def input_gradient(dkv, dq, w_all):
    quarter = w_all.shape[1]
    d = quarter // 4
    any_space = pl.BlockSpec(memory_space=pl.ANY)
    vmem = pl.BlockSpec(memory_space=pltpu.VMEM)
    dma = pltpu.SemaphoreType.DMA
    chunk = (4, HD, 2 * HD)
    half = (2, HD, 2 * HD)
    return pl.pallas_call(
        gradient_kernel,
        name="input_gradient",
        out_shape=jax.ShapeDtypeStruct((2 * HD, d), BF16),
        in_specs=[vmem, vmem, any_space],
        out_specs=vmem,
        scratch_shapes=[
            pltpu.VMEM(w_all.shape, BF16),
            pltpu.VMEM((4, 4 * HD, 3 * HD), BF16),
            pltpu.VMEM((1,) + chunk, BF16),
            pltpu.VMEM((4,) + chunk, BF16),
            pltpu.VMEM((2, 2) + half, BF16),
            pltpu.VMEM((2,) + half, BF16),
            pltpu.VMEM((2,) + half, BF16),
            pltpu.VMEM((2, 2) + half, BF16),
            pltpu.VMEM((2,) + half, F32),
            pltpu.VMEM((6, 2 * HD, d), BF16),
            pltpu.VMEM((6, 2 * HD, d), BF16),
            pltpu.VMEM((2, 2 * HD, d), F32),
            pltpu.VMEM((2, 2 * HD, d), BF16),
            pltpu.VMEM((2, 2, HD, d), BF16),
            dma((32,)), dma, dma((4,)), dma((2,)), dma((2, 2)), dma((4,)), dma((4,)),
            dma((2,)), dma((4,)), dma((2, 2)),
        ],
        compiler_params=pltpu.CompilerParams(
            collective_id=1, has_side_effects=True, vmem_limit_bytes=VMEM_BYTES
        ),
    )(dkv, dq, w_all)


def shards(inputs, w_qkv, selected, d_attn):
    w3 = w_qkv.transpose(1, 0, 2)
    q, kv, do, w_all = project_and_gather(inputs, w3, d_attn)
    dq, dkv = attend(
        selected, q.reshape(4, HD, HD), kv.reshape(8, BLOCK, 2 * HD), do
    )
    return input_gradient(dkv.reshape(4, 4, 2, HD, 2 * HD), dq.reshape(4 * HD, HD), w_all)


def solution(mesh):
    placed = (P("ctx", None), P("ctx", None, "fsdp"), P(), P("ctx", "fsdp"))
    return jax.shard_map(
        shards, mesh=mesh, in_specs=placed, out_specs=P("ctx", "fsdp"), check_vma=False
    )
```

time: 631 us -> 174 us (0.28)
  the two profiles are of different devices: /device:TPU:97 before, /device:TPU:9 now
where the time goes in v1:
time: 174 us
  Pallas kernels  170 us (98%)
  local copies, waits for them, and re-layouts  3.12 us (2%)
    pallas_call x1, Pallas kernels, input_gradient(): pl.pallas_call(gradient_kernel, name='input_gradient', out_shape=jax.Shap...  85.1 us
    pallas_call x1, Pallas kernels, project_and_gather(): pl.pallas_call(project_kernel, name='project_and_gather', out_shape=(jax....  74.9 us
    pallas_call x1, Pallas kernels, attend(): pl.pallas_call(attend_kernel, name='attend', out_shape=(jax.ShapeDtypeStr...  10.4 us

profile of v1, /device:TPU:9, one launch (start us, length us, event | category | flops | bytes accessed | tf_op | source)
XLA Modules:
  0.0 173.5 jit_solution(11571636743824098577)
XLA Ops:
  0.0 1.3 copy.5.selected
  1.3 74.9 %project_and_gather.1 = (bf16[512,128]{1,0:T(8,128)(2,1)}, bf16[4,4,2,128,256]{4,3,2,1,0:T(8,128)(2,1)}, bf16[4,128,128]{2,1,0:T(8,128)(2,1)}, bf16[4,1792,384]{2,1,0:T(8,128)(2,1)}) custom-call(bf16[256,7168]{1,0:T(8,128)(2,1)} %inp.1, bf16[3,448,256]{2,1,0:T(8,128)(2,1)} %bitcast.7, bf16[256,256]{1,0:T(8,128)(2,1)} %d_attn.1), custom_call_target="tpu_custom_call" | custom-call | tf_op jit(solution)/shard_map/project_and_gather/pallas_call | solution.py:295
  76.2 10.4 %attend.1 = (bf16[4,128,128]{2,1,0:T(8,128)(2,1)}, bf16[8,512,256]{2,1,0:T(8,128)(2,1)}) custom-call(s32[8,4]{1,0:T(8,128)} %copy.5.selected, bf16[4,128,128]{2,1,0:T(8,128)(2,1)} %bitcast.9, bf16[8,512,256]{2,1,0:T(8,128)(2,1)} %bitcast.5, bf16[4,128,128]{2,1,0:T(8,128)(2,1)} %get-tuple-element.13.do_ref), custom_call_target="tpu_custom_call" | custom-call | tf_op jit(solution)/shard_map/attend/pallas_call | solution.py:380
  86.7 85.1 %input_gradient.1 = bf16[256,448]{1,0:T(8,128)(2,1)} custom-call(bf16[4,4,2,128,256]{4,3,2,1,0:T(8,128)(2,1)} %bitcast.6, bf16[512,128]{1,0:T(8,128)(2,1)} %bitcast.8, bf16[4,1792,384]{2,1,0:T(8,128)(2,1)} %get-tuple-element.16.w_in), custom_call_target="tpu_custom_call" | custom-call | tf_op jit(solution)/shard_map/input_gradient/pallas_call | solution.py:553
  171.8 1.8 %copy.6 = bf16[256,448]{0,1:T(8,128)(2,1)} copy(bf16[256,448]{1,0:T(8,128)(2,1)} %input_gradient.1) | data formatting | bytes 458752 | tf_op jit(solution)/shard_map/input_gradient/pallas_call | solution.py:553

commit v2 on v1

v2 whole, which is shorter than its diff:
```python
import functools

import jax
import jax.numpy as jnp
from jax import lax
from jax.experimental import pallas as pl
from jax.experimental.pallas import tpu as pltpu
from jax.sharding import PartitionSpec as P

MESH = pl.DeviceIdType.MESH
F32 = jnp.float32
BF16 = jnp.bfloat16
HD = 128
BLOCK = 512
TOP = 4
SCALE = HD ** (-0.5)
VMEM_BYTES = 60 * 1024 * 1024


def place():
    c = lax.axis_index("ctx")
    f = lax.axis_index("fsdp")
    return (
        lax.div(c, 4), lax.rem(c, 4),
        lax.div(f, 8), lax.rem(lax.div(f, 2), 4), lax.rem(f, 2),
    )


def device(z, y, zh, x, k):
    return (z * 4 + y, zh * 8 + x * 2 + k)


def turn(i, by):
    return lax.rem(i + by, 4)


def rows(start, size):
    return pl.ds(pl.multiple_of(start, size & -size), size)


class Mail:
    def __init__(self, send_sems):
        self.send_sems = send_sems
        self.used = 0
        self.sent = []

    def copy(self, src, dst, recv, dev):
        sem = self.send_sems.at[self.used]
        self.used += 1
        return pltpu.make_async_remote_copy(
            src_ref=src, dst_ref=dst, send_sem=sem, recv_sem=recv,
            device_id=dev, device_id_type=MESH,
        )

    def send(self, src, dst, recv, dev):
        copy = self.copy(src, dst, recv, dev)
        copy.start()
        self.sent.append((copy, None, None))

    def send_or_keep(self, away, src, dst, recv, dev):
        copy = self.copy(src, dst, recv, dev)
        stay = pltpu.make_async_copy(src, dst, recv)

        @pl.when(away)
        def _():
            copy.start()

        @pl.when(jnp.logical_not(away))
        def _():
            stay.start()

        self.sent.append((copy, away, None))

    def send_if(self, away, src, dst, recv, dev):
        copy = self.copy(src, dst, recv, dev)

        @pl.when(away)
        def _():
            copy.start()

        self.sent.append((copy, away, None))

    def flush(self):
        for copy, away, _ in self.sent:
            if away is None:
                copy.wait_send()
            else:
                pl.when(away)(copy.wait_send)


def got(dst, recv):
    pltpu.make_async_copy(dst, dst, recv).wait()


class Ring:
    def __init__(self, mail, view, pos, core, right, left, partner, ring, cores):
        self.mail, self.view, self.pos, self.core = mail, view, pos, core
        self.right, self.left, self.partner = right, left, partner
        self.ring, self.cores = ring, cores

    def pass_on(self, pos, half, recv, dev):
        ref = self.view(self.core, pos, half)
        self.mail.send(ref, ref, recv, dev)

    def across(self, pos, half, n):
        if self.partner is not None:
            self.pass_on(pos, half, self.cores.at[n], self.partner)

    def start(self):
        self.pass_on(self.pos, None, self.ring.at[0], self.right)
        self.pass_on(self.pos, None, self.ring.at[1], self.left)
        self.across(self.pos, None, 0)

    def relay(self):
        before, after = turn(self.pos, 3), turn(self.pos, 1)
        got(self.view(self.core, before, None), self.ring.at[0])
        self.pass_on(before, 0, self.ring.at[2], self.right)
        self.across(before, None, 1)
        got(self.view(self.core, after, None), self.ring.at[1])
        self.pass_on(after, 1, self.ring.at[3], self.left)
        self.across(after, None, 2)

    def finish(self):
        far = turn(self.pos, 2)
        for half in (0, 1):
            got(self.view(self.core, far, half), self.ring.at[2 + half])
            self.across(far, half, 3 + half)

    def settle(self):
        other = 1 - self.core
        before, after, far = turn(self.pos, 3), turn(self.pos, 1), turn(self.pos, 2)
        got(self.view(other, self.pos, None), self.cores.at[0])
        got(self.view(other, before, None), self.cores.at[1])
        got(self.view(other, after, None), self.cores.at[2])
        got(self.view(other, far, 0), self.cores.at[3])
        got(self.view(other, far, 1), self.cores.at[4])


def enter(devices, more=0):
    barrier = pltpu.get_barrier_semaphore()
    for dev in devices:
        pl.semaphore_signal(barrier, inc=1, device_id=dev, device_id_type=MESH)
    return barrier, len(devices) + more


def project_kernel(
    inp, w3, d_attn, q_out, kv_out, do_out, w_out,
    wall, xall, dall, part, parts_in, via_in, own, kvall,
    send_sems, load_sems, w_ring, w_cores, x_z, x_ring, d_sems, p_sems, via_sems,
    kv_ring, kv_cores, out_sems,
):
    z, y, zh, x, j = place()
    partner = device(z, y, zh, x, 1 - j)
    right = device(z, turn(y, 1), zh, x, j)
    left = device(z, turn(y, 3), zh, x, j)
    dq = wall.shape[1]
    d = dq // 4
    up = z >= 2
    end = jnp.logical_or(z == 0, z == 3)
    mid = jnp.logical_not(end)
    flip = lambda h: jnp.where(up, h, 3 - h)
    heads = (
        flip(jnp.where(end, 0, 2)), flip(jnp.where(end, 2, 0)), flip(1), flip(3),
    )
    inner = jnp.where(up, 2, 1)
    first = jnp.where(up, 0, 1)
    kv_cols, q_cols = pl.ds(0, 2 * HD), pl.ds(2 * HD, HD)

    loads = []
    for n, s in enumerate((first, 1 - first)):
        for at in (0, 1):
            loads.append(pltpu.make_async_copy(
                w3.at[1 + at, :, rows(HD * s, HD)],
                wall.at[2 * j + s, rows(d * y, d), pl.ds(HD * at, HD)],
                load_sems.at[2 * n + at],
            ))
    for s in (0, 1):
        loads.append(pltpu.make_async_copy(
            w3.at[0, :, pl.ds(HD * s, HD)],
            wall.at[2 * j + s, rows(d * y, d), q_cols],
            load_sems.at[4 + s],
        ))
    own_x = pltpu.make_async_copy(
        inp.at[rows(HD * j, HD), rows(dq * z, dq)], xall.at[pl.ds(0, HD)], load_sems.at[6]
    )
    for copy in loads:
        copy.start()
    own_x.start()

    peers = [device(turn(z, t), y, zh, x, k) for t in (1, 2, 3) for k in (j, 1 - j)]
    peers += [partner, right, left]
    peers += [device(z, y, zh, turn(x, u), j) for u in (1, 3)]
    barrier, expected = enter(peers)
    pl.semaphore_wait(barrier, expected)

    mail = Mail(send_sems)

    def w_view(s):
        def view(core, pos, half):
            if half is None:
                return wall.at[2 * core + s, rows(d * pos, d), kv_cols]
            return wall.at[2 * core + s, rows(d * pos + (d // 2) * half, d // 2), kv_cols]
        return view

    def q_view(core, pos, half):
        if half is None:
            return wall.at[pl.ds(2 * core, 2), rows(d * pos, d), q_cols]
        return wall.at[pl.ds(2 * core, 2), rows(d * pos + (d // 2) * half, d // 2), q_cols]

    w_rings = [
        Ring(mail, view, y, j, right, left, partner, w_ring.at[n], w_cores.at[n])
        for n, view in enumerate((w_view(first), w_view(1 - first), q_view))
    ]
    piece = HD // 4

    def x_view(t):
        def view(core, pos, half):
            if half is None:
                return xall.at[rows(HD * t + piece * pos, piece)]
            return xall.at[rows(HD * t + piece * pos + (piece // 2) * half, piece // 2)]
        return view

    x_rings = {
        t: Ring(
            mail, x_view(t), x, j, device(z, y, zh, turn(x, 1), j),
            device(z, y, zh, turn(x, 3), j), None, x_ring.at[t - 1], None,
        )
        for t in (1, 2, 3)
    }

    blocks = ((0, HD, 0, 2 * HD), (HD, 3 * HD, 0, 2 * HD), (0, 4 * HD, 2 * HD, HD))

    def project(p, i):
        low, size, col, wide = blocks[i]
        at, cols = pl.ds(low, size), pl.ds(col, wide)
        head = heads[p]
        total = jnp.dot(xall[at], wall[head, :, cols], preferred_element_type=F32)
        mine = part.at[p, at, cols]

        def keep():
            own[at, cols] = total

        def store():
            part[p, at, cols] = total.astype(BF16)

        def store_both():
            for n in ((0, 1), (), (2,))[i]:
                first_row, length, *_ = blocks[n]
                got(via_in.at[pl.ds(first_row, length), cols], via_sems.at[n])
            for t in range(low // HD, (low + size) // HD):
                there_t = turn(t, jnp.where(up, 3, 1))
                part[p, pl.ds(HD * t, HD), cols] = (
                    total[HD * t - low : HD * (t + 1) - low]
                    + via_in[rows(HD * there_t, HD), cols].astype(F32)
                ).astype(BF16)

        there = parts_in.at[z, at, cols]
        target = device(head, y, zh, x, j)
        if p == 0:
            pl.when(end)(store)
            pl.when(mid)(keep)
            mail.send_if(
                end, mine, via_in.at[at, cols], via_sems.at[i], device(inner, y, zh, x, j)
            )
        elif p == 1:
            pl.when(end)(store)
            pl.when(mid)(store_both)
            mail.send(mine, there, p_sems.at[z, i], target)
        elif p == 2:
            store()
            mail.send(mine, there, p_sems.at[z, i], target)
        else:
            pl.when(mid)(store)
            pl.when(end)(keep)
            mail.send_if(mid, mine, there, p_sems.at[z, i], target)

    for copy in loads[:2]:
        copy.wait()
    w_rings[0].start()
    for t in (1, 3, 2):
        zd = turn(z, t)
        back = 4 - t
        mail.send(
            inp.at[rows(HD * j + piece * x, piece), rows(dq * zd, dq)],
            xall.at[rows(HD * back + piece * x, piece)],
            x_z.at[back - 1], device(zd, y, zh, x, j),
        )
    for copy in loads[2:]:
        copy.wait()
    w_rings[0].relay()
    w_rings[1].start()
    for t in (1, 3, 2):
        got(xall.at[rows(HD * t + piece * x, piece)], x_z.at[t - 1])
        x_rings[t].start()
    own_x.wait()
    w_rings[0].finish()
    w_rings[0].settle()
    project(0, 0)
    for t in (1, 3, 2):
        x_rings[t].relay()
    w_rings[1].relay()
    w_rings[2].start()
    for t in (1, 3, 2):
        x_rings[t].finish()
    project(0, 1)
    project(1, 0)
    project(1, 1)
    w_rings[1].finish()
    w_rings[1].settle()
    project(2, 0)
    project(2, 1)
    project(3, 0)
    project(3, 1)
    w_rings[2].relay()
    w_rings[2].finish()
    w_rings[2].settle()
    keep_w = pltpu.make_async_copy(wall, w_out, out_sems.at[0])
    keep_w.start()
    for p in range(4):
        project(p, 2)
    for s in (0, 1):
        for k in (0, 1):
            zd = 2 * j + s
            away = jnp.logical_or(zd != z, j != k)
            mail.send_or_keep(
                away,
                d_attn.at[pl.ds(HD * k, HD), pl.ds(HD * s, HD)],
                dall.at[z], d_sems.at[z], device(zd, y, zh, x, k),
            )

    one = jnp.where(z == 1, 2, 1)
    two = jnp.where(end, 2, 0)

    def collect(which, cols, put):
        def arrived(source):
            for i in which:
                low, size, col, wide = blocks[i]
                got(parts_in.at[source, pl.ds(low, size), pl.ds(col, wide)], p_sems.at[source, i])

        def total(run):
            at = lambda source: rows(HD * lax.rem(run + 4 - source, 4), HD)
            term = lambda source: parts_in[source, at(source), cols].astype(F32)
            return own[at(z), cols] + term(one) + term(two), term

        arrived(one)
        arrived(two)

        @pl.when(mid)
        def _():
            arrived(3)
            for run in range(4):
                base, term = total(run)
                put(run, (base + term(3)).astype(BF16))

        @pl.when(end)
        def _():
            for run in range(4):
                put(run, total(run)[0].astype(BF16))

    def put_kv(run, low):
        kvall[run, y, j] = low

    def put_q(run, low):
        q_out[run] = low

    def kv_view(core, pos, half):
        if half is None:
            return kvall.at[:, pos, core]
        return kvall.at[pl.ds(2 * half, 2), pos, core]

    kv = Ring(mail, kv_view, y, j, right, left, partner, kv_ring, kv_cores)
    collect((0, 1), kv_cols, put_kv)
    kv.start()
    for zs in range(4):
        got(dall.at[zs], d_sems.at[zs])
    do_out[...] = dall[...]
    kv.relay()
    collect((2,), q_cols, put_q)
    kv.finish()
    kv.settle()
    keep_kv = pltpu.make_async_copy(kvall, kv_out, out_sems.at[1])
    keep_kv.start()
    mail.flush()
    keep_w.wait()
    keep_kv.wait()


def project_and_gather(inputs, w3, d_attn):
    rows_here, width = inputs.shape
    quarter = width // 4
    any_space = pl.BlockSpec(memory_space=pl.ANY)
    vmem = pl.BlockSpec(memory_space=pltpu.VMEM)
    dma = pltpu.SemaphoreType.DMA
    return pl.pallas_call(
        project_kernel,
        name="project_and_gather",
        out_shape=(
            jax.ShapeDtypeStruct((4, HD, HD), BF16),
            jax.ShapeDtypeStruct((4, 4, 2, HD, 2 * HD), BF16),
            jax.ShapeDtypeStruct((4, HD, HD), BF16),
            jax.ShapeDtypeStruct((4, quarter, 3 * HD), BF16),
        ),
        in_specs=[any_space] * 3,
        out_specs=(vmem, any_space, vmem, any_space),
        scratch_shapes=[
            pltpu.VMEM((4, quarter, 3 * HD), BF16),
            pltpu.VMEM((4 * HD, quarter), BF16),
            pltpu.VMEM((4, HD, HD), BF16),
            pltpu.VMEM((4, 4 * HD, 3 * HD), BF16),
            pltpu.VMEM((4, 4 * HD, 3 * HD), BF16),
            pltpu.VMEM((4 * HD, 3 * HD), BF16),
            pltpu.VMEM((4 * HD, 3 * HD), F32),
            pltpu.VMEM((4, 4, 2, HD, 2 * HD), BF16),
            dma((72,)), dma((7,)), dma((3, 4)), dma((3, 5)), dma((3,)), dma((3, 4)),
            dma((4,)), dma((4, 3)), dma((3,)), dma((4,)), dma((5,)), dma((2,)),
        ],
        compiler_params=pltpu.CompilerParams(
            collective_id=0, has_side_effects=True, vmem_limit_bytes=VMEM_BYTES
        ),
    )(inputs, w3, d_attn)


def attend_kernel(selected, q_ref, kv_ref, do_ref, dq_ref, dkv_ref, score, soft, total):
    _, y, _, _, j = place()
    total[...] = jnp.zeros_like(total)
    contract = lambda a, b: (((a,), (b,)), ((), ()))
    dot = functools.partial(lax.dot_general, preferred_element_type=F32)
    key_at = lax.broadcasted_iota(jnp.int32, (BLOCK, HD), 0)
    query_at = lax.broadcasted_iota(jnp.int32, (BLOCK, HD), 1)

    def tile(run, carry):
        first = (run * 4 + y) * 256 + HD * j
        block = lax.div(first, BLOCK)
        q = q_ref[run]
        do = do_ref[run]
        highest = jnp.full((1, HD), -jnp.inf, F32)
        for t in range(TOP):
            chosen = selected[t, block]
            kb = jnp.maximum(chosen, 0)
            s = dot(kv_ref[kb, :, :HD], q, contract(1, 1)) * SCALE
            limit = jnp.where(chosen >= 0, first - kb * BLOCK, -2 * BLOCK)
            s = jnp.where(key_at - query_at <= limit, s, -jnp.inf)
            score[t] = s
            highest = jnp.maximum(highest, jnp.max(s, axis=0, keepdims=True))
        totals = jnp.zeros((1, HD), F32)
        for t in range(TOP):
            e = jnp.exp(score[t] - highest)
            score[t] = e
            totals += jnp.sum(e, axis=0, keepdims=True)
        share = 1.0 / totals
        attended = jnp.zeros((HD, HD), F32)
        for t in range(TOP):
            kb = jnp.maximum(selected[t, block], 0)
            p = score[t] * share
            low = p.astype(BF16)
            score[t] = p
            soft[t] = low
            attended += dot(kv_ref[kb, :, HD:], low, contract(0, 0))
        attended = attended.astype(BF16).astype(F32)
        delta = jnp.sum(do.astype(F32).T * attended, axis=0, keepdims=True)
        dq = jnp.zeros((HD, HD), F32)
        for t in range(TOP):
            kb = jnp.maximum(selected[t, block], 0)
            dp = dot(kv_ref[kb, :, HD:], do, contract(1, 1))
            ds = (score[t] * (dp - delta)).astype(BF16)
            total[kb, :, :HD] += dot(ds, q, contract(1, 0))
            total[kb, :, HD:] += dot(soft[t], do, contract(1, 0))
            dq += dot(ds, kv_ref[kb, :, :HD], contract(0, 0))
        dq_ref[run] = (dq * SCALE).astype(BF16)
        return carry

    lax.fori_loop(0, 4, tile, 0)
    for b in range(8):
        dkv_ref[b, :, :HD] = (total[b, :, :HD] * SCALE).astype(BF16)
        dkv_ref[b, :, HD:] = total[b, :, HD:].astype(BF16)


def attend(selected, q, kv, do):
    vmem = pl.BlockSpec(memory_space=pltpu.VMEM)
    return pl.pallas_call(
        attend_kernel,
        name="attend",
        out_shape=(
            jax.ShapeDtypeStruct((4, HD, HD), BF16),
            jax.ShapeDtypeStruct((8, BLOCK, 2 * HD), BF16),
        ),
        in_specs=[pl.BlockSpec(memory_space=pltpu.SMEM), vmem, vmem, vmem],
        out_specs=(vmem, vmem),
        scratch_shapes=[
            pltpu.VMEM((TOP, BLOCK, HD), F32),
            pltpu.VMEM((TOP, BLOCK, HD), BF16),
            pltpu.VMEM((8, BLOCK, 2 * HD), F32),
        ],
        compiler_params=pltpu.CompilerParams(vmem_limit_bytes=VMEM_BYTES),
    )(selected, q, kv, do)


def owner_x(z, jj):
    at = jnp.where(lax.rem(jj, 2) == 0, lax.div(jj, 2), lax.div(7 - jj, 2))
    return turn(at, 2 * lax.rem(z, 2))


def block_of(z, x):
    at = turn(x, 2 * lax.rem(z, 2))
    return jnp.where(at < 2, 2 * at, 7 - 2 * at)


def gradient_kernel(
    dkv, dq, w_in, out,
    wall, gall, core_in, far_out, near_out, far_in, near_in, own_kv,
    xf_out, xn_out, xf_in, xn_in, own_x, fin, fin_in,
    send_sems, load_sem, core_sems, far_sems, near_sems, q_sems, g_sems, xf_sems, xn_sems, f_sems,
):
    z, y, zh, x, j = place()
    d = wall.shape[1] // 4
    f = lax.axis_index("fsdp")
    partner = device(z, y, zh, x, 1 - j)
    right = device(z, turn(y, 1), zh, x, j)
    left = device(z, turn(y, 3), zh, x, j)
    x_right = device(z, y, zh, turn(x, 1), j)
    x_left = device(z, y, zh, turn(x, 3), j)
    up = z >= 2
    end = jnp.logical_or(z == 0, z == 3)
    mid = jnp.logical_not(end)
    flip = lambda h: jnp.where(up, h, 3 - h)
    at_z = lambda h: device(h, y, zh, x, j)
    first_z = flip(jnp.where(end, 2, 1))
    second_z = flip(jnp.where(end, 1, 3))
    far_z = flip(0)

    load = pltpu.make_async_copy(w_in, wall, load_sem)
    load.start()

    across = [at_z(turn(z, t)) for t in (1, 2, 3)]
    barrier, expected = enter([partner, right, left, x_right, x_left] + across, more=4)
    source_z = lax.div(f, 4)
    source_x = owner_x(source_z, lax.rem(f, 4))
    for h in (0, 1):
        for k in (0, 1):
            pl.semaphore_signal(
                barrier, inc=1, device_id=device(source_z, y, h, source_x, k),
                device_id_type=MESH,
            )
    pl.semaphore_wait(barrier, expected)

    mail = Mail(send_sems)

    def spread(src, at, cols, sems):
        there = gall.at[z, at, cols]
        mail.send(src, there, sems.at[z], at_z(first_z))
        mail.send_if(mid, src, there, sems.at[z], at_z(far_z))
        mail.send(src, there, sems.at[z], at_z(second_z))

    def forward(at, cols, sems):
        block = gall.at[far_z, at, cols]
        pl.when(mid)(lambda: got(block, sems.at[far_z]))
        mail.send_if(mid, block, block, sems.at[far_z], at_z(second_z))

    def gathered(at, cols, sems):
        for h in (flip(1), flip(2)):
            pl.when(h != z)(lambda: got(gall.at[h, at, cols], sems.at[h]))
        outer = jnp.where(end, 3 - z, second_z)
        got(gall.at[outer, at, cols], sems.at[outer])

    every, q_cols, kv_cols = pl.ds(0, 4 * HD), pl.ds(2 * HD, HD), pl.ds(0, 2 * HD)
    for n, t in enumerate((2, 1, 3, 0)):
        mail.send(dkv.at[:, turn(y, t), 1 - j], core_in.at[n], core_sems.at[n], partner)
    spread(dq, every, q_cols, q_sems)
    gall[z, :, q_cols] = dq[...]

    def chip_sum(n, t, run):
        return dkv[run, turn(y, t), j].astype(F32) + core_in[n, run].astype(F32)

    def far(h):
        for side, dev in ((0, right), (1, left)):
            far_out[h, side] = chip_sum(0, 2, 2 * h + side).astype(BF16)
            mail.send(far_out.at[h, side], far_in.at[h, side], far_sems.at[h, side], dev)

    def near(h, term):
        for side, (t, dev) in enumerate(((1, right), (3, left))):
            lane = side if term else 1 - side
            total = chip_sum(1 + side, t, 2 * h + lane)
            if term:
                got(far_in.at[h, side], far_sems.at[h, side])
                total += far_in[h, side].astype(F32)
            near_out[h, side, lane] = total.astype(BF16)
            mail.send(
                near_out.at[h, side, lane], near_in.at[h, side, lane],
                near_sems.at[h, side, lane], dev,
            )

    def finish_kv(h):
        for lane in (0, 1):
            for side in (1 - lane, lane):
                got(near_in.at[h, side, lane], near_sems.at[h, side, lane])
        for lane in (0, 1):
            run = 2 * h + lane
            total = chip_sum(3, 0, run)
            for side in (0, 1):
                total += near_in[h, side, lane].astype(F32)
            gall[z, pl.ds(HD * run, HD), kv_cols] = total.astype(BF16)
        at = pl.ds(2 * HD * h, 2 * HD)
        spread(gall.at[z, at, kv_cols], at, kv_cols, g_sems.at[h])

    got(core_in.at[0], core_sems.at[0])
    far(0)
    got(core_in.at[1], core_sems.at[1])
    got(core_in.at[2], core_sems.at[2])
    near(0, False)
    far(1)
    got(core_in.at[3], core_sems.at[3])
    near(0, True)
    near(1, False)
    forward(every, q_cols, q_sems)
    finish_kv(0)
    near(1, True)
    finish_kv(1)

    def part(t, h):
        cols = rows(d * block_of(z, turn(x, t)), d)
        at = pl.ds(2 * HD * h, 2 * HD)
        total = jnp.zeros((d, 2 * HD), F32)
        for head in range(4):
            total += lax.dot_general(
                wall[head, cols], gall[head, at], (((1,), (1,)), ((), ())),
                preferred_element_type=F32,
            )
        return total

    def x_first(h):
        total = part(2, h).astype(BF16)
        for side, dev in ((0, x_right), (1, x_left)):
            xf_out[h, side] = total[:, HD * side : HD * (side + 1)]
            mail.send(xf_out.at[h, side], xf_in.at[h, side], xf_sems.at[h, side], dev)
        for side, (t, dev) in enumerate(((1, x_right), (3, x_left))):
            total = part(t, h)
            alone = 1 - side
            xn_out[h, side, alone] = total[:, HD * alone : HD * (alone + 1)].astype(BF16)
            own_x[h, side] = total[:, HD * side : HD * (side + 1)]
            mail.send(
                xn_out.at[h, side, alone], xn_in.at[h, side, alone],
                xn_sems.at[h, side, alone], dev,
            )

    def x_second(h):
        for side, dev in ((0, x_right), (1, x_left)):
            got(xf_in.at[h, side], xf_sems.at[h, side])
            xn_out[h, side, side] = (
                own_x[h, side] + xf_in[h, side].astype(F32)
            ).astype(BF16)
            mail.send(
                xn_out.at[h, side, side], xn_in.at[h, side, side], xn_sems.at[h, side, side], dev
            )
        total = part(0, h)
        for lane in (0, 1):
            own_x[h, lane] = total[:, HD * lane : HD * (lane + 1)]

    fd = 4 * z + block_of(z, x)

    def x_third(h):
        for lane in (0, 1):
            total = own_x[h, lane]
            for side in (1 - lane, lane):
                got(xn_in.at[h, side, lane], xn_sems.at[h, side, lane])
                total += xn_in[h, side, lane].astype(F32)
            run = 2 * h + lane
            fin[run] = total.astype(BF16)
            mail.send_or_keep(
                jnp.logical_or(run != z, fd != f), fin.at[run], fin_in.at[zh, j],
                f_sems.at[zh, j], (run * 4 + y, fd),
            )

    load.wait()
    gathered(every, q_cols, q_sems)
    halves = [pl.ds(2 * HD * h, 2 * HD) for h in (0, 1)]
    forward(halves[0], kv_cols, g_sems.at[0])
    gathered(halves[0], kv_cols, g_sems.at[0])
    x_first(0)
    forward(halves[1], kv_cols, g_sems.at[1])
    x_second(0)
    gathered(halves[1], kv_cols, g_sems.at[1])
    x_first(1)
    x_third(0)
    x_second(1)
    x_third(1)
    for h in (0, 1):
        for k in (0, 1):
            got(fin_in.at[h, k], f_sems.at[h, k])
    for k in (0, 1):
        out[pl.ds(HD * k, HD)] = (
            (fin_in[0, k].astype(F32) + fin_in[1, k].astype(F32)).T
        ).astype(BF16)
    mail.flush()


def input_gradient(dkv, dq, w_all):
    quarter = w_all.shape[1]
    d = quarter // 4
    any_space = pl.BlockSpec(memory_space=pl.ANY)
    vmem = pl.BlockSpec(memory_space=pltpu.VMEM)
    dma = pltpu.SemaphoreType.DMA
    run = (HD, 2 * HD)
    block = (d, HD)
    return pl.pallas_call(
        gradient_kernel,
        name="input_gradient",
        out_shape=jax.ShapeDtypeStruct((2 * HD, d), BF16),
        in_specs=[vmem, vmem, any_space],
        out_specs=vmem,
        scratch_shapes=[
            pltpu.VMEM(w_all.shape, BF16),
            pltpu.VMEM((4, 4 * HD, 3 * HD), BF16),
            pltpu.VMEM((4, 4) + run, BF16),
            pltpu.VMEM((2, 2) + run, BF16),
            pltpu.VMEM((2, 2, 2) + run, BF16),
            pltpu.VMEM((2, 2) + run, BF16),
            pltpu.VMEM((2, 2, 2) + run, BF16),
            pltpu.VMEM((2, 2) + run, F32),
            pltpu.VMEM((2, 2) + block, BF16),
            pltpu.VMEM((2, 2, 2) + block, BF16),
            pltpu.VMEM((2, 2) + block, BF16),
            pltpu.VMEM((2, 2, 2) + block, BF16),
            pltpu.VMEM((2, 2) + block, F32),
            pltpu.VMEM((4,) + block, BF16),
            pltpu.VMEM((2, 2) + block, BF16),
            dma((48,)), dma, dma((4,)), dma((2, 2)), dma((2, 2, 2)), dma((4,)), dma((2, 4)),
            dma((2, 2)), dma((2, 2, 2)), dma((2, 2)),
        ],
        compiler_params=pltpu.CompilerParams(
            collective_id=1, has_side_effects=True, vmem_limit_bytes=VMEM_BYTES
        ),
    )(dkv, dq, w_all)


def shards(inputs, w_qkv, selected, d_attn):
    w3 = w_qkv.transpose(1, 0, 2)
    q, kv, do, w_all = project_and_gather(inputs, w3, d_attn)
    dq, dkv = attend(
        selected.T, q, kv.reshape(8, BLOCK, 2 * HD), do
    )
    return input_gradient(dkv.reshape(4, 4, 2, HD, 2 * HD), dq.reshape(4 * HD, HD), w_all)


def solution(mesh):
    placed = (P("ctx", None), P("ctx", None, "fsdp"), P(), P("ctx", "fsdp"))
    return jax.shard_map(
        shards, mesh=mesh, in_specs=placed, out_specs=P("ctx", "fsdp"), check_vma=False
    )
```

time: 174 us -> 150 us (0.86)
  the two profiles are of different devices: /device:TPU:9 before, /device:TPU:97 now
where the time goes in v2:
time: 150 us
  Pallas kernels  148 us (99%)
  local copies, waits for them, and re-layouts  1.78 us (1%)
    pallas_call x1, Pallas kernels, project_and_gather(): pl.pallas_call(project_kernel, name='project_and_gather', out_shape=(jax....  72 us
    pallas_call x1, Pallas kernels, input_gradient(): pl.pallas_call(gradient_kernel, name='input_gradient', out_shape=jax.Shap...  65.6 us
    pallas_call x1, Pallas kernels, attend(): pl.pallas_call(attend_kernel, name='attend', out_shape=(jax.ShapeDtypeStr...  10.4 us

profile of v2, /device:TPU:97, one launch (start us, length us, event | category | flops | bytes accessed | tf_op | source)
XLA Modules:
  0.0 149.8 jit_solution(8864964501080169454)
XLA Ops:
  0.0 72.0 %project_and_gather.1 = (bf16[4,128,128]{2,1,0:T(8,128)(2,1)}, bf16[4,4,2,128,256]{4,3,2,1,0:T(8,128)(2,1)}, bf16[4,128,128]{2,1,0:T(8,128)(2,1)}, bf16[4,1792,384]{2,1,0:T(8,128)(2,1)}) custom-call(bf16[256,7168]{1,0:T(8,128)(2,1)} %inp.1, bf16[3,448,256]{2,1,0:T(8,128)(2,1)} %bitcast.7, bf16[256,256]{1,0:T(8,128)(2,1)} %d_attn.1), custom_call_target="tpu_custom_call" | custom-call | tf_op jit(solution)/shard_map/project_and_gather/pallas_call | solution.py:394
  72.0 10.4 %attend.1 = (bf16[4,128,128]{2,1,0:T(8,128)(2,1)}, bf16[8,512,256]{2,1,0:T(8,128)(2,1)}) custom-call(s32[4,8]{1,0:T(4,128)} %bitcast.9, bf16[4,128,128]{2,1,0:T(8,128)(2,1)} %get-tuple-element.11.q_ref, bf16[8,512,256]{2,1,0:T(8,128)(2,1)} %bitcast.5, bf16[4,128,128]{2,1,0:T(8,128)(2,1)} %get-tuple-element.13.do_ref), custom_call_target="tpu_custom_call" | custom-call | tf_op jit(solution)/shard_map/attend/pallas_call | solution.py:480
  82.4 65.6 %input_gradient.1 = bf16[256,448]{1,0:T(8,128)(2,1)} custom-call(bf16[4,4,2,128,256]{4,3,2,1,0:T(8,128)(2,1)} %bitcast.6, bf16[512,128]{1,0:T(8,128)(2,1)} %bitcast.8, bf16[4,1792,384]{2,1,0:T(8,128)(2,1)} %get-tuple-element.16.w_in), custom_call_target="tpu_custom_call" | custom-call | tf_op jit(solution)/shard_map/input_gradient/pallas_call | solution.py:704
  148.0 1.8 %copy.5 = bf16[256,448]{0,1:T(8,128)(2,1)} copy(bf16[256,448]{1,0:T(8,128)(2,1)} %input_gradient.1) | data formatting | bytes 458752 | tf_op jit(solution)/shard_map/input_gradient/pallas_call | solution.py:704

commit v3 on v2

--- a/solution.py
+++ b/solution.py
@@ -30,6 +30,11 @@
     return (z * 4 + y, zh * 8 + x * 2 + k)
 
 
+def around(z, y, zh, x, k, by):
+    at = lax.rem(4 * zh + z + 8 + by, 8)
+    return device(lax.rem(at, 4), y, lax.div(at, 4), x, k)
+
+
 def turn(i, by):
     return lax.rem(i + by, 4)
 
@@ -146,7 +151,7 @@
 def project_kernel(
     inp, w3, d_attn, q_out, kv_out, do_out, w_out,
     wall, xall, dall, part, parts_in, via_in, own, kvall,
-    send_sems, load_sems, w_ring, w_cores, x_z, x_ring, d_sems, p_sems, via_sems,
+    send_sems, load_sems, w_ring, w_cores, x_z, x_x, d_sems, p_sems, via_sems,
     kv_ring, kv_cores, out_sems,
 ):
     z, y, zh, x, j = place()
@@ -181,7 +186,7 @@
             load_sems.at[4 + s],
         ))
     own_x = pltpu.make_async_copy(
-        inp.at[rows(HD * j, HD), rows(dq * z, dq)], xall.at[pl.ds(0, HD)], load_sems.at[6]
+        inp.at[rows(HD * j, HD), rows(dq * z, dq)], xall.at[rows(HD * z, HD)], load_sems.at[6]
     )
     for copy in loads:
         copy.start()
@@ -190,6 +195,7 @@
     peers = [device(turn(z, t), y, zh, x, k) for t in (1, 2, 3) for k in (j, 1 - j)]
     peers += [partner, right, left]
     peers += [device(z, y, zh, turn(x, u), j) for u in (1, 3)]
+    peers += [around(z, y, zh, x, j, by) for by in (1, -1, 2, -2)]
     barrier, expected = enter(peers)
     pl.semaphore_wait(barrier, expected)
 
@@ -213,22 +219,38 @@
     ]
     piece = HD // 4
 
-    def x_view(t):
-        def view(core, pos, half):
-            if half is None:
-                return xall.at[rows(HD * t + piece * pos, piece)]
-            return xall.at[rows(HD * t + piece * pos + (piece // 2) * half, piece // 2)]
-        return view
-
-    x_rings = {
-        t: Ring(
-            mail, x_view(t), x, j, device(z, y, zh, turn(x, 1), j),
-            device(z, y, zh, turn(x, 3), j), None, x_ring.at[t - 1], None,
-        )
-        for t in (1, 2, 3)
-    }
-
-    blocks = ((0, HD, 0, 2 * HD), (HD, 3 * HD, 0, 2 * HD), (0, 4 * HD, 2 * HD, HD))
+    def quarter(run, of_x, low=0, size=piece):
+        return xall.at[rows(HD * run + piece * of_x + low, size)]
+
+    hops = ((1, 0, piece), (-1, 0, piece), (2, 0, piece // 2), (-2, piece // 2, piece // 2))
+    opposite = turn(x, 2)
+
+    def x_send(turn_of):
+        of_x = (x, opposite)[turn_of]
+        for n, (by, low, size) in enumerate(hops):
+            mail.send(
+                inp.at[rows(HD * j + piece * of_x + low, size), rows(dq * turn(z, 4 + by), dq)],
+                quarter(z, of_x, low, size), x_z.at[turn_of, n], around(z, y, zh, x, j, by),
+            )
+
+    def x_got(turn_of, n):
+        by, low, size = hops[n]
+        got(quarter(turn(z, 4 - by), (x, opposite)[turn_of], low, size), x_z.at[turn_of, n])
+
+    def x_share(by):
+        mine = quarter(turn(z, 4 - by), x)
+        for u in (1, 3):
+            mail.send(
+                mine, mine, x_x.at[by % 4, u // 2], device(z, y, zh, turn(x, u), j)
+            )
+
+    def x_shared(by):
+        for u in (1, 3):
+            got(quarter(turn(z, 4 - by), turn(x, 4 - u)), x_x.at[by % 4, u // 2])
+
+    blocks = (
+        (0, 2 * HD, 0, 2 * HD), (2 * HD, 2 * HD, 0, 2 * HD), (0, 4 * HD, 2 * HD, HD),
+    )
 
     def project(p, i):
         low, size, col, wide = blocks[i]
@@ -244,15 +266,8 @@
             part[p, at, cols] = total.astype(BF16)
 
         def store_both():
-            for n in ((0, 1), (), (2,))[i]:
-                first_row, length, *_ = blocks[n]
-                got(via_in.at[pl.ds(first_row, length), cols], via_sems.at[n])
-            for t in range(low // HD, (low + size) // HD):
-                there_t = turn(t, jnp.where(up, 3, 1))
-                part[p, pl.ds(HD * t, HD), cols] = (
-                    total[HD * t - low : HD * (t + 1) - low]
-                    + via_in[rows(HD * there_t, HD), cols].astype(F32)
-                ).astype(BF16)
+            got(via_in.at[at, cols], via_sems.at[i])
+            part[p, at, cols] = (total + via_in[at, cols].astype(F32)).astype(BF16)
 
         there = parts_in.at[z, at, cols]
         target = device(head, y, zh, x, j)
@@ -277,41 +292,36 @@
     for copy in loads[:2]:
         copy.wait()
     w_rings[0].start()
-    for t in (1, 3, 2):
-        zd = turn(z, t)
-        back = 4 - t
-        mail.send(
-            inp.at[rows(HD * j + piece * x, piece), rows(dq * zd, dq)],
-            xall.at[rows(HD * back + piece * x, piece)],
-            x_z.at[back - 1], device(zd, y, zh, x, j),
-        )
+    x_send(0)
+    x_send(1)
     for copy in loads[2:]:
         copy.wait()
+    for n, by in ((0, 1), (1, -1)):
+        x_got(0, n)
+        x_share(by)
     w_rings[0].relay()
     w_rings[1].start()
-    for t in (1, 3, 2):
-        got(xall.at[rows(HD * t + piece * x, piece)], x_z.at[t - 1])
-        x_rings[t].start()
+    w_rings[2].start()
+    x_got(0, 2)
+    x_got(0, 3)
+    x_share(2)
     own_x.wait()
     w_rings[0].finish()
     w_rings[0].settle()
-    project(0, 0)
-    for t in (1, 3, 2):
-        x_rings[t].relay()
+    for by in (1, -1, 2):
+        x_shared(by)
+    for n in range(4):
+        x_got(1, n)
+    for i in (0, 1):
+        project(0, i)
+        project(1, i)
     w_rings[1].relay()
-    w_rings[2].start()
-    for t in (1, 3, 2):
-        x_rings[t].finish()
-    project(0, 1)
-    project(1, 0)
-    project(1, 1)
     w_rings[1].finish()
+    w_rings[2].relay()
     w_rings[1].settle()
-    project(2, 0)
-    project(2, 1)
-    project(3, 0)
-    project(3, 1)
-    w_rings[2].relay()
+    for i in (0, 1):
+        project(2, i)
+        project(3, i)
     w_rings[2].finish()
     w_rings[2].settle()
     keep_w = pltpu.make_async_copy(wall, w_out, out_sems.at[0])
@@ -331,53 +341,57 @@
     one = jnp.where(z == 1, 2, 1)
     two = jnp.where(end, 2, 0)
 
-    def collect(which, cols, put):
-        def arrived(source):
-            for i in which:
-                low, size, col, wide = blocks[i]
-                got(parts_in.at[source, pl.ds(low, size), pl.ds(col, wide)], p_sems.at[source, i])
-
-        def total(run):
-            at = lambda source: rows(HD * lax.rem(run + 4 - source, 4), HD)
-            term = lambda source: parts_in[source, at(source), cols].astype(F32)
-            return own[at(z), cols] + term(one) + term(two), term
-
+    def collect(i, put):
+        low, size, col, wide = blocks[i]
+        at, cols = pl.ds(low, size), pl.ds(col, wide)
+        arrived = lambda source: got(parts_in.at[source, at, cols], p_sems.at[source, i])
+        term = lambda source: parts_in[source, at, cols].astype(F32)
         arrived(one)
         arrived(two)
 
         @pl.when(mid)
         def _():
             arrived(3)
-            for run in range(4):
-                base, term = total(run)
-                put(run, (base + term(3)).astype(BF16))
+            put((own[at, cols] + term(one) + term(two) + term(3)).astype(BF16))
 
         @pl.when(end)
         def _():
-            for run in range(4):
-                put(run, total(run)[0].astype(BF16))
-
-    def put_kv(run, low):
-        kvall[run, y, j] = low
-
-    def put_q(run, low):
-        q_out[run] = low
-
-    def kv_view(core, pos, half):
-        if half is None:
-            return kvall.at[:, pos, core]
-        return kvall.at[pl.ds(2 * half, 2), pos, core]
-
-    kv = Ring(mail, kv_view, y, j, right, left, partner, kv_ring, kv_cores)
-    collect((0, 1), kv_cols, put_kv)
-    kv.start()
+            put((own[at, cols] + term(one) + term(two)).astype(BF16))
+
+    def put_kv(h):
+        def put(low):
+            for run in (0, 1):
+                kvall[2 * h + run, y, j] = low[HD * run : HD * (run + 1)]
+        return put
+
+    def put_q(low):
+        for run in range(4):
+            q_out[run] = low[HD * run : HD * (run + 1)]
+
+    def kv_view(h):
+        def view(core, pos, half):
+            if half is None:
+                return kvall.at[pl.ds(2 * h, 2), pos, core]
+            return kvall.at[pl.ds(2 * h + half, 1), pos, core]
+        return view
+
+    kv = [
+        Ring(mail, kv_view(h), y, j, right, left, partner, kv_ring.at[h], kv_cores.at[h])
+        for h in (0, 1)
+    ]
+    for h in (0, 1):
+        collect(h, put_kv(h))
+        kv[h].start()
+    for h in (0, 1):
+        kv[h].relay()
     for zs in range(4):
         got(dall.at[zs], d_sems.at[zs])
     do_out[...] = dall[...]
-    kv.relay()
-    collect((2,), q_cols, put_q)
-    kv.finish()
-    kv.settle()
+    collect(2, put_q)
+    for h in (0, 1):
+        kv[h].finish()
+    for h in (0, 1):
+        kv[h].settle()
     keep_kv = pltpu.make_async_copy(kvall, kv_out, out_sems.at[1])
     keep_kv.start()
     mail.flush()
@@ -411,8 +425,8 @@
             pltpu.VMEM((4 * HD, 3 * HD), BF16),
             pltpu.VMEM((4 * HD, 3 * HD), F32),
             pltpu.VMEM((4, 4, 2, HD, 2 * HD), BF16),
-            dma((72,)), dma((7,)), dma((3, 4)), dma((3, 5)), dma((3,)), dma((3, 4)),
-            dma((4,)), dma((4, 3)), dma((3,)), dma((4,)), dma((5,)), dma((2,)),
+            dma((80,)), dma((7,)), dma((3, 4)), dma((3, 5)), dma((2, 4)), dma((4, 2)),
+            dma((4,)), dma((4, 3)), dma((3,)), dma((2, 4)), dma((2, 5)), dma((2,)),
         ],
         compiler_params=pltpu.CompilerParams(
             collective_id=0, has_side_effects=True, vmem_limit_bytes=VMEM_BYTES

time: 150 us -> 140 us (0.933)
  Pallas kernels: 148 us -> 137 us
    pallas_call x1, Pallas kernels: 72 us -> 62.8 us  [project_and_gather(): pl.pallas_call(project_kernel, name='project_and_gather', out_shape=(jax....]
where the time goes in v3:
time: 140 us; the launch traced here: 139 us
  Pallas kernels  137 us (98%)
  local copies, waits for them, and re-layouts  1.78 us (1%)
    pallas_call x1, Pallas kernels, input_gradient(): pl.pallas_call(gradient_kernel, name='input_gradient', out_shape=jax.Shap...  64.3 us
    pallas_call x1, Pallas kernels, project_and_gather(): pl.pallas_call(project_kernel, name='project_and_gather', out_shape=(jax....  62.8 us
    pallas_call x1, Pallas kernels, attend(): pl.pallas_call(attend_kernel, name='attend', out_shape=(jax.ShapeDtypeStr...  10.4 us

profile of v3, /device:TPU:97, one launch (start us, length us, event | category | flops | bytes accessed | tf_op | source)
XLA Modules:
  0.0 139.3 jit_solution(4528057456295310021)
XLA Ops:
  0.0 62.8 %project_and_gather.1 = (bf16[4,128,128]{2,1,0:T(8,128)(2,1)}, bf16[4,4,2,128,256]{4,3,2,1,0:T(8,128)(2,1)}, bf16[4,128,128]{2,1,0:T(8,128)(2,1)}, bf16[4,1792,384]{2,1,0:T(8,128)(2,1)}) custom-call(bf16[256,7168]{1,0:T(8,128)(2,1)} %inp.1, bf16[3,448,256]{2,1,0:T(8,128)(2,1)} %bitcast.7, bf16[256,256]{1,0:T(8,128)(2,1)} %d_attn.1), custom_call_target="tpu_custom_call" | custom-call | tf_op jit(solution)/shard_map/project_and_gather/pallas_call | solution.py:408
  62.8 10.4 %attend.1 = (bf16[4,128,128]{2,1,0:T(8,128)(2,1)}, bf16[8,512,256]{2,1,0:T(8,128)(2,1)}) custom-call(s32[4,8]{1,0:T(4,128)} %bitcast.9, bf16[4,128,128]{2,1,0:T(8,128)(2,1)} %get-tuple-element.11.q_ref, bf16[8,512,256]{2,1,0:T(8,128)(2,1)} %bitcast.5, bf16[4,128,128]{2,1,0:T(8,128)(2,1)} %get-tuple-element.13.do_ref), custom_call_target="tpu_custom_call" | custom-call | tf_op jit(solution)/shard_map/attend/pallas_call | solution.py:494
  73.2 64.3 %input_gradient.1 = bf16[256,448]{1,0:T(8,128)(2,1)} custom-call(bf16[4,4,2,128,256]{4,3,2,1,0:T(8,128)(2,1)} %bitcast.6, bf16[512,128]{1,0:T(8,128)(2,1)} %bitcast.8, bf16[4,1792,384]{2,1,0:T(8,128)(2,1)} %get-tuple-element.16.w_in), custom_call_target="tpu_custom_call" | custom-call | tf_op jit(solution)/shard_map/input_gradient/pallas_call | solution.py:718
  137.5 1.8 %copy.5 = bf16[256,448]{0,1:T(8,128)(2,1)} copy(bf16[256,448]{1,0:T(8,128)(2,1)} %input_gradient.1) | data formatting | bytes 458752 | tf_op jit(solution)/shard_map/input_gradient/pallas_call | solution.py:718

commit v4 on v3

--- a/solution.py
+++ b/solution.py
@@ -164,27 +164,18 @@
     end = jnp.logical_or(z == 0, z == 3)
     mid = jnp.logical_not(end)
     flip = lambda h: jnp.where(up, h, 3 - h)
-    heads = (
-        flip(jnp.where(end, 0, 2)), flip(jnp.where(end, 2, 0)), flip(1), flip(3),
-    )
-    inner = jnp.where(up, 2, 1)
-    first = jnp.where(up, 0, 1)
-    kv_cols, q_cols = pl.ds(0, 2 * HD), pl.ds(2 * HD, HD)
+    heads = tuple(flip(jnp.where(end, p, (p + 3) % 4)) for p in range(4))
+    inside = device(jnp.where(up, 2, 1), y, zh, x, j)
+    kinds = [pl.ds(HD * i, HD) for i in range(3)]
 
     loads = []
-    for n, s in enumerate((first, 1 - first)):
-        for at in (0, 1):
+    for i, p in enumerate((1, 2, 0)):
+        for s in (0, 1):
             loads.append(pltpu.make_async_copy(
-                w3.at[1 + at, :, rows(HD * s, HD)],
-                wall.at[2 * j + s, rows(d * y, d), pl.ds(HD * at, HD)],
-                load_sems.at[2 * n + at],
+                w3.at[p, :, pl.ds(HD * s, HD)],
+                wall.at[2 * j + s, rows(d * y, d), kinds[i]],
+                load_sems.at[2 * i + s],
             ))
-    for s in (0, 1):
-        loads.append(pltpu.make_async_copy(
-            w3.at[0, :, pl.ds(HD * s, HD)],
-            wall.at[2 * j + s, rows(d * y, d), q_cols],
-            load_sems.at[4 + s],
-        ))
     own_x = pltpu.make_async_copy(
         inp.at[rows(HD * j, HD), rows(dq * z, dq)], xall.at[rows(HD * z, HD)], load_sems.at[6]
     )
@@ -201,21 +192,18 @@
 
     mail = Mail(send_sems)
 
-    def w_view(s):
+    def w_view(i):
         def view(core, pos, half):
             if half is None:
-                return wall.at[2 * core + s, rows(d * pos, d), kv_cols]
-            return wall.at[2 * core + s, rows(d * pos + (d // 2) * half, d // 2), kv_cols]
+                return wall.at[pl.ds(2 * core, 2), rows(d * pos, d), kinds[i]]
+            return wall.at[
+                pl.ds(2 * core, 2), rows(d * pos + (d // 2) * half, d // 2), kinds[i]
+            ]
         return view
 
-    def q_view(core, pos, half):
-        if half is None:
-            return wall.at[pl.ds(2 * core, 2), rows(d * pos, d), q_cols]
-        return wall.at[pl.ds(2 * core, 2), rows(d * pos + (d // 2) * half, d // 2), q_cols]
-
     w_rings = [
-        Ring(mail, view, y, j, right, left, partner, w_ring.at[n], w_cores.at[n])
-        for n, view in enumerate((w_view(first), w_view(1 - first), q_view))
+        Ring(mail, w_view(i), y, j, right, left, partner, w_ring.at[i], w_cores.at[i])
+        for i in range(3)
     ]
     piece = HD // 4
 
@@ -248,46 +236,40 @@
         for u in (1, 3):
             got(quarter(turn(z, 4 - by), turn(x, 4 - u)), x_x.at[by % 4, u // 2])
 
-    blocks = (
-        (0, 2 * HD, 0, 2 * HD), (2 * HD, 2 * HD, 0, 2 * HD), (0, 4 * HD, 2 * HD, HD),
-    )
-
-    def project(p, i):
-        low, size, col, wide = blocks[i]
-        at, cols = pl.ds(low, size), pl.ds(col, wide)
-        head = heads[p]
-        total = jnp.dot(xall[at], wall[head, :, cols], preferred_element_type=F32)
-        mine = part.at[p, at, cols]
-
-        def keep():
-            own[at, cols] = total
-
-        def store():
-            part[p, at, cols] = total.astype(BF16)
-
-        def store_both():
-            got(via_in.at[at, cols], via_sems.at[i])
-            part[p, at, cols] = (total + via_in[at, cols].astype(F32)).astype(BF16)
-
-        there = parts_in.at[z, at, cols]
-        target = device(head, y, zh, x, j)
-        if p == 0:
-            pl.when(end)(store)
-            pl.when(mid)(keep)
-            mail.send_if(
-                end, mine, via_in.at[at, cols], via_sems.at[i], device(inner, y, zh, x, j)
-            )
-        elif p == 1:
-            pl.when(end)(store)
-            pl.when(mid)(store_both)
-            mail.send(mine, there, p_sems.at[z, i], target)
-        elif p == 2:
-            store()
-            mail.send(mine, there, p_sems.at[z, i], target)
-        else:
-            pl.when(mid)(store)
-            pl.when(end)(keep)
-            mail.send_if(mid, mine, there, p_sems.at[z, i], target)
+    def project(i):
+        cols = kinds[i]
+        for p in range(4):
+            head = heads[p]
+            if p % 2 == 0:
+                both = jnp.dot(
+                    xall[...],
+                    jnp.concatenate([wall[head, :, cols], wall[heads[p + 1], :, cols]], axis=1),
+                    preferred_element_type=F32,
+                )
+            total = both[:, HD * (p % 2) : HD * (p % 2 + 1)]
+            if p == 3:
+                own[:, cols] = total
+                continue
+            mine = part.at[p, :, cols]
+            there = parts_in.at[z, :, cols]
+
+            def store():
+                part[p, :, cols] = total.astype(BF16)
+
+            def store_both():
+                got(via_in.at[p - 1, :, cols], via_sems.at[p - 1, i])
+                part[p, :, cols] = (total + via_in[p - 1, :, cols].astype(F32)).astype(BF16)
+
+            if p == 0:
+                store()
+            else:
+                pl.when(end)(store)
+                pl.when(mid)(store_both)
+            if p < 2:
+                mail.send_if(end, mine, via_in.at[p, :, cols], via_sems.at[p, i], inside)
+                mail.send_if(mid, mine, there, p_sems.at[z, i], device(head, y, zh, x, j))
+            else:
+                mail.send(mine, there, p_sems.at[z, i], device(head, y, zh, x, j))
 
     for copy in loads[:2]:
         copy.wait()
@@ -301,7 +283,6 @@
         x_share(by)
     w_rings[0].relay()
     w_rings[1].start()
-    w_rings[2].start()
     x_got(0, 2)
     x_got(0, 3)
     x_share(2)
@@ -312,22 +293,48 @@
         x_shared(by)
     for n in range(4):
         x_got(1, n)
-    for i in (0, 1):
-        project(0, i)
-        project(1, i)
     w_rings[1].relay()
+    w_rings[2].start()
+    project(0)
     w_rings[1].finish()
+    w_rings[1].settle()
+    project(1)
     w_rings[2].relay()
-    w_rings[1].settle()
-    for i in (0, 1):
-        project(2, i)
-        project(3, i)
+
+    one = jnp.where(z == 1, 2, 1)
+    two = jnp.where(end, 2, jnp.where(up, 3, 0))
+
+    def collect(i):
+        cols = kinds[i]
+        total = own[:, cols]
+        for source in (one, two):
+            got(parts_in.at[source, :, cols], p_sems.at[source, i])
+            total += parts_in[source, :, cols].astype(F32)
+        low = total.astype(BF16)
+        for run in range(4):
+            if i == 2:
+                q_out[run] = low[HD * run : HD * (run + 1)]
+            else:
+                kvall[run, y, j, :, cols] = low[HD * run : HD * (run + 1)]
+
+    def kv_view(i):
+        def view(core, pos, half):
+            if half is None:
+                return kvall.at[:, pos, core, :, kinds[i]]
+            return kvall.at[pl.ds(2 * half, 2), pos, core, :, kinds[i]]
+        return view
+
+    kv = [
+        Ring(mail, kv_view(i), y, j, right, left, partner, kv_ring.at[i], kv_cores.at[i])
+        for i in (0, 1)
+    ]
+    collect(0)
+    kv[0].start()
     w_rings[2].finish()
     w_rings[2].settle()
     keep_w = pltpu.make_async_copy(wall, w_out, out_sems.at[0])
     keep_w.start()
-    for p in range(4):
-        project(p, 2)
+    project(2)
     for s in (0, 1):
         for k in (0, 1):
             zd = 2 * j + s
@@ -338,60 +345,18 @@
                 dall.at[z], d_sems.at[z], device(zd, y, zh, x, k),
             )
 
-    one = jnp.where(z == 1, 2, 1)
-    two = jnp.where(end, 2, 0)
-
-    def collect(i, put):
-        low, size, col, wide = blocks[i]
-        at, cols = pl.ds(low, size), pl.ds(col, wide)
-        arrived = lambda source: got(parts_in.at[source, at, cols], p_sems.at[source, i])
-        term = lambda source: parts_in[source, at, cols].astype(F32)
-        arrived(one)
-        arrived(two)
-
-        @pl.when(mid)
-        def _():
-            arrived(3)
-            put((own[at, cols] + term(one) + term(two) + term(3)).astype(BF16))
-
-        @pl.when(end)
-        def _():
-            put((own[at, cols] + term(one) + term(two)).astype(BF16))
-
-    def put_kv(h):
-        def put(low):
-            for run in (0, 1):
-                kvall[2 * h + run, y, j] = low[HD * run : HD * (run + 1)]
-        return put
-
-    def put_q(low):
-        for run in range(4):
-            q_out[run] = low[HD * run : HD * (run + 1)]
-
-    def kv_view(h):
-        def view(core, pos, half):
-            if half is None:
-                return kvall.at[pl.ds(2 * h, 2), pos, core]
-            return kvall.at[pl.ds(2 * h + half, 1), pos, core]
-        return view
-
-    kv = [
-        Ring(mail, kv_view(h), y, j, right, left, partner, kv_ring.at[h], kv_cores.at[h])
-        for h in (0, 1)
-    ]
-    for h in (0, 1):
-        collect(h, put_kv(h))
-        kv[h].start()
-    for h in (0, 1):
-        kv[h].relay()
+    kv[0].relay()
+    collect(1)
+    kv[1].start()
+    kv[0].finish()
+    kv[1].relay()
     for zs in range(4):
         got(dall.at[zs], d_sems.at[zs])
     do_out[...] = dall[...]
-    collect(2, put_q)
-    for h in (0, 1):
-        kv[h].finish()
-    for h in (0, 1):
-        kv[h].settle()
+    collect(2)
+    kv[1].finish()
+    for i in (0, 1):
+        kv[i].settle()
     keep_kv = pltpu.make_async_copy(kvall, kv_out, out_sems.at[1])
     keep_kv.start()
     mail.flush()
@@ -422,11 +387,11 @@
             pltpu.VMEM((4, HD, HD), BF16),
             pltpu.VMEM((4, 4 * HD, 3 * HD), BF16),
             pltpu.VMEM((4, 4 * HD, 3 * HD), BF16),
-            pltpu.VMEM((4 * HD, 3 * HD), BF16),
+            pltpu.VMEM((2, 4 * HD, 3 * HD), BF16),
             pltpu.VMEM((4 * HD, 3 * HD), F32),
             pltpu.VMEM((4, 4, 2, HD, 2 * HD), BF16),
             dma((80,)), dma((7,)), dma((3, 4)), dma((3, 5)), dma((2, 4)), dma((4, 2)),
-            dma((4,)), dma((4, 3)), dma((3,)), dma((2, 4)), dma((2, 5)), dma((2,)),
+            dma((4,)), dma((4, 3)), dma((2, 3)), dma((2, 4)), dma((2, 5)), dma((2,)),
         ],
         compiler_params=pltpu.CompilerParams(
             collective_id=0, has_side_effects=True, vmem_limit_bytes=VMEM_BYTES
@@ -562,19 +527,24 @@
     def spread(src, at, cols, sems):
         there = gall.at[z, at, cols]
         mail.send(src, there, sems.at[z], at_z(first_z))
-        mail.send_if(mid, src, there, sems.at[z], at_z(far_z))
         mail.send(src, there, sems.at[z], at_z(second_z))
 
     def forward(at, cols, sems):
-        block = gall.at[far_z, at, cols]
-        pl.when(mid)(lambda: got(block, sems.at[far_z]))
-        mail.send_if(mid, block, block, sems.at[far_z], at_z(second_z))
+        for h in (first_z, far_z):
+            block = gall.at[h, at, cols]
+            pl.when(mid)(lambda: got(block, sems.at[h]))
+            mail.send_if(mid, block, block, sems.at[h], at_z(second_z))
 
     def gathered(at, cols, sems):
-        for h in (flip(1), flip(2)):
-            pl.when(h != z)(lambda: got(gall.at[h, at, cols], sems.at[h]))
-        outer = jnp.where(end, 3 - z, second_z)
-        got(gall.at[outer, at, cols], sems.at[outer])
+        def wait(h):
+            got(gall.at[h, at, cols], sems.at[h])
+
+        wait(second_z)
+
+        @pl.when(end)
+        def _():
+            wait(first_z)
+            wait(3 - z)
 
     every, q_cols, kv_cols = pl.ds(0, 4 * HD), pl.ds(2 * HD, HD), pl.ds(0, 2 * HD)
     for n, t in enumerate((2, 1, 3, 0)):

time: 140 us -> 137 us (0.979)
  Pallas kernels: 137 us -> 135 us
    pallas_call x1, Pallas kernels: 62.8 us -> 59.6 us  [project_and_gather(): pl.pallas_call(project_kernel, name='project_and_gather', out_shape=(jax....]
where the time goes in v4:
time: 137 us
  Pallas kernels  135 us (99%)
  local copies, waits for them, and re-layouts  1.78 us (1%)
    pallas_call x1, Pallas kernels, input_gradient(): pl.pallas_call(gradient_kernel, name='input_gradient', out_shape=jax.Shap...  64.8 us
    pallas_call x1, Pallas kernels, project_and_gather(): pl.pallas_call(project_kernel, name='project_and_gather', out_shape=(jax....  59.6 us
    pallas_call x1, Pallas kernels, attend(): pl.pallas_call(attend_kernel, name='attend', out_shape=(jax.ShapeDtypeStr...  10.4 us

profile of v4, /device:TPU:97, one launch (start us, length us, event | category | flops | bytes accessed | tf_op | source)
XLA Modules:
  0.0 136.6 jit_solution(14764748675641639299)
XLA Ops:
  0.0 59.6 %project_and_gather.1 = (bf16[4,128,128]{2,1,0:T(8,128)(2,1)}, bf16[4,4,2,128,256]{4,3,2,1,0:T(8,128)(2,1)}, bf16[4,128,128]{2,1,0:T(8,128)(2,1)}, bf16[4,1792,384]{2,1,0:T(8,128)(2,1)}) custom-call(bf16[256,7168]{1,0:T(8,128)(2,1)} %inp.1, bf16[3,448,256]{2,1,0:T(8,128)(2,1)} %bitcast.7, bf16[256,256]{1,0:T(8,128)(2,1)} %d_attn.1), custom_call_target="tpu_custom_call" | custom-call | tf_op jit(solution)/shard_map/project_and_gather/pallas_call | solution.py:373
  59.6 10.4 %attend.1 = (bf16[4,128,128]{2,1,0:T(8,128)(2,1)}, bf16[8,512,256]{2,1,0:T(8,128)(2,1)}) custom-call(s32[4,8]{1,0:T(4,128)} %bitcast.9, bf16[4,128,128]{2,1,0:T(8,128)(2,1)} %get-tuple-element.11.q_ref, bf16[8,512,256]{2,1,0:T(8,128)(2,1)} %bitcast.5, bf16[4,128,128]{2,1,0:T(8,128)(2,1)} %get-tuple-element.13.do_ref), custom_call_target="tpu_custom_call" | custom-call | tf_op jit(solution)/shard_map/attend/pallas_call | solution.py:459
  70.0 64.8 %input_gradient.1 = bf16[256,448]{1,0:T(8,128)(2,1)} custom-call(bf16[4,4,2,128,256]{4,3,2,1,0:T(8,128)(2,1)} %bitcast.6, bf16[512,128]{1,0:T(8,128)(2,1)} %bitcast.8, bf16[4,1792,384]{2,1,0:T(8,128)(2,1)} %get-tuple-element.16.w_in), custom_call_target="tpu_custom_call" | custom-call | tf_op jit(solution)/shard_map/input_gradient/pallas_call | solution.py:688
  134.8 1.8 %copy.5 = bf16[256,448]{0,1:T(8,128)(2,1)} copy(bf16[256,448]{1,0:T(8,128)(2,1)} %input_gradient.1) | data formatting | bytes 458752 | tf_op jit(solution)/shard_map/input_gradient/pallas_call | solution.py:688

commit v5 on v4

--- a/solution.py
+++ b/solution.py
@@ -14,6 +14,7 @@
 BLOCK = 512
 TOP = 4
 SCALE = HD ** (-0.5)
+AHEAD = 2
 VMEM_BYTES = 60 * 1024 * 1024
 
 
@@ -486,7 +487,7 @@
 
 def gradient_kernel(
     dkv, dq, w_in, out,
-    wall, gall, core_in, far_out, near_out, far_in, near_in, own_kv,
+    wall, gall, core_in, far_out, near_out, far_in, near_in,
     xf_out, xn_out, xf_in, xn_in, own_x, fin, fin_in,
     send_sems, load_sem, core_sems, far_sems, near_sems, q_sems, g_sems, xf_sems, xn_sems, f_sems,
 ):
@@ -546,6 +547,7 @@
             wait(first_z)
             wait(3 - z)
 
+    runs = [pl.ds(HD * r, HD) for r in range(4)]
     every, q_cols, kv_cols = pl.ds(0, 4 * HD), pl.ds(2 * HD, HD), pl.ds(0, 2 * HD)
     for n, t in enumerate((2, 1, 3, 0)):
         mail.send(dkv.at[:, turn(y, t), 1 - j], core_in.at[n], core_sems.at[n], partner)
@@ -573,6 +575,10 @@
                 near_sems.at[h, side, lane], dev,
             )
 
+    def spread_run(run):
+        at = runs[run]
+        spread(gall.at[z, at, kv_cols], at, kv_cols, g_sems.at[run])
+
     def finish_kv(h):
         for lane in (0, 1):
             for side in (1 - lane, lane):
@@ -582,9 +588,10 @@
             total = chip_sum(3, 0, run)
             for side in (0, 1):
                 total += near_in[h, side, lane].astype(F32)
-            gall[z, pl.ds(HD * run, HD), kv_cols] = total.astype(BF16)
-        at = pl.ds(2 * HD * h, 2 * HD)
-        spread(gall.at[z, at, kv_cols], at, kv_cols, g_sems.at[h])
+            at = runs[run]
+            gall[z, at, kv_cols] = total.astype(BF16)
+            if run < AHEAD:
+                spread_run(run)
 
     got(core_in.at[0], core_sems.at[0])
     far(0)
@@ -600,73 +607,72 @@
     near(1, True)
     finish_kv(1)
 
-    def part(t, h):
+    def part(t, r):
         cols = rows(d * block_of(z, turn(x, t)), d)
-        at = pl.ds(2 * HD * h, 2 * HD)
-        total = jnp.zeros((d, 2 * HD), F32)
+        total = jnp.zeros((d, HD), F32)
         for head in range(4):
             total += lax.dot_general(
-                wall[head, cols], gall[head, at], (((1,), (1,)), ((), ())),
+                wall[head, cols], gall[head, runs[r]], (((1,), (1,)), ((), ())),
                 preferred_element_type=F32,
             )
-        return total
-
-    def x_first(h):
-        total = part(2, h).astype(BF16)
+        return total[: d // 2], total[d // 2 :]
+
+    def x_first(r):
+        total = part(2, r)
         for side, dev in ((0, x_right), (1, x_left)):
-            xf_out[h, side] = total[:, HD * side : HD * (side + 1)]
-            mail.send(xf_out.at[h, side], xf_in.at[h, side], xf_sems.at[h, side], dev)
+            xf_out[r, side] = total[side].astype(BF16)
+            mail.send(xf_out.at[r, side], xf_in.at[r, side], xf_sems.at[r, side], dev)
         for side, (t, dev) in enumerate(((1, x_right), (3, x_left))):
-            total = part(t, h)
+            total = part(t, r)
             alone = 1 - side
-            xn_out[h, side, alone] = total[:, HD * alone : HD * (alone + 1)].astype(BF16)
-            own_x[h, side] = total[:, HD * side : HD * (side + 1)]
+            xn_out[r, side, alone] = total[alone].astype(BF16)
+            own_x[r, side] = total[side]
             mail.send(
-                xn_out.at[h, side, alone], xn_in.at[h, side, alone],
-                xn_sems.at[h, side, alone], dev,
+                xn_out.at[r, side, alone], xn_in.at[r, side, alone],
+                xn_sems.at[r, side, alone], dev,
             )
 
-    def x_second(h):
+    def x_second(r):
         for side, dev in ((0, x_right), (1, x_left)):
-            got(xf_in.at[h, side], xf_sems.at[h, side])
-            xn_out[h, side, side] = (
-                own_x[h, side] + xf_in[h, side].astype(F32)
+            got(xf_in.at[r, side], xf_sems.at[r, side])
+            xn_out[r, side, side] = (
+                own_x[r, side] + xf_in[r, side].astype(F32)
             ).astype(BF16)
             mail.send(
-                xn_out.at[h, side, side], xn_in.at[h, side, side], xn_sems.at[h, side, side], dev
+                xn_out.at[r, side, side], xn_in.at[r, side, side], xn_sems.at[r, side, side], dev
             )
-        total = part(0, h)
+        total = part(0, r)
         for lane in (0, 1):
-            own_x[h, lane] = total[:, HD * lane : HD * (lane + 1)]
+            own_x[r, lane] = total[lane]
 
     fd = 4 * z + block_of(z, x)
 
-    def x_third(h):
+    def x_third(r):
         for lane in (0, 1):
-            total = own_x[h, lane]
+            total = own_x[r, lane]
             for side in (1 - lane, lane):
-                got(xn_in.at[h, side, lane], xn_sems.at[h, side, lane])
-                total += xn_in[h, side, lane].astype(F32)
-            run = 2 * h + lane
-            fin[run] = total.astype(BF16)
-            mail.send_or_keep(
-                jnp.logical_or(run != z, fd != f), fin.at[run], fin_in.at[zh, j],
-                f_sems.at[zh, j], (run * 4 + y, fd),
-            )
+                got(xn_in.at[r, side, lane], xn_sems.at[r, side, lane])
+                total += xn_in[r, side, lane].astype(F32)
+            fin[r, pl.ds((d // 2) * lane, d // 2)] = total.astype(BF16)
+        mail.send_or_keep(
+            jnp.logical_or(r != z, fd != f), fin.at[r], fin_in.at[zh, j],
+            f_sems.at[zh, j], (r * 4 + y, fd),
+        )
 
     load.wait()
     gathered(every, q_cols, q_sems)
-    halves = [pl.ds(2 * HD * h, 2 * HD) for h in (0, 1)]
-    forward(halves[0], kv_cols, g_sems.at[0])
-    gathered(halves[0], kv_cols, g_sems.at[0])
-    x_first(0)
-    forward(halves[1], kv_cols, g_sems.at[1])
-    x_second(0)
-    gathered(halves[1], kv_cols, g_sems.at[1])
-    x_first(1)
-    x_third(0)
-    x_second(1)
-    x_third(1)
+    for r in range(4):
+        forward(runs[r], kv_cols, g_sems.at[r])
+        if r + AHEAD < 4:
+            spread_run(r + AHEAD)
+        if r >= 1:
+            x_second(r - 1)
+        gathered(runs[r], kv_cols, g_sems.at[r])
+        x_first(r)
+        if r >= 1:
+            x_third(r - 1)
+    x_second(3)
+    x_third(3)
     for h in (0, 1):
         for k in (0, 1):
             got(fin_in.at[h, k], f_sems.at[h, k])
@@ -684,7 +690,7 @@
     vmem = pl.BlockSpec(memory_space=pltpu.VMEM)
     dma = pltpu.SemaphoreType.DMA
     run = (HD, 2 * HD)
-    block = (d, HD)
+    block, lane = (d, HD), (d // 2, HD)
     return pl.pallas_call(
         gradient_kernel,
         name="input_gradient",
@@ -699,16 +705,15 @@
             pltpu.VMEM((2, 2, 2) + run, BF16),
             pltpu.VMEM((2, 2) + run, BF16),
             pltpu.VMEM((2, 2, 2) + run, BF16),
-            pltpu.VMEM((2, 2) + run, F32),
-            pltpu.VMEM((2, 2) + block, BF16),
-            pltpu.VMEM((2, 2, 2) + block, BF16),
-            pltpu.VMEM((2, 2) + block, BF16),
-            pltpu.VMEM((2, 2, 2) + block, BF16),
-            pltpu.VMEM((2, 2) + block, F32),
+            pltpu.VMEM((4, 2) + lane, BF16),
+            pltpu.VMEM((4, 2, 2) + lane, BF16),
+            pltpu.VMEM((4, 2) + lane, BF16),
+            pltpu.VMEM((4, 2, 2) + lane, BF16),
+            pltpu.VMEM((4, 2) + lane, F32),
             pltpu.VMEM((4,) + block, BF16),
             pltpu.VMEM((2, 2) + block, BF16),
-            dma((48,)), dma, dma((4,)), dma((2, 2)), dma((2, 2, 2)), dma((4,)), dma((2, 4)),
-            dma((2, 2)), dma((2, 2, 2)), dma((2, 2)),
+            dma((72,)), dma, dma((4,)), dma((2, 2)), dma((2, 2, 2)), dma((4,)), dma((4, 4)),
+            dma((4, 2)), dma((4, 2, 2)), dma((2, 2)),
         ],
         compiler_params=pltpu.CompilerParams(
             collective_id=1, has_side_effects=True, vmem_limit_bytes=VMEM_BYTES

time: 137 us -> 135 us (0.985)
  Pallas kernels: 135 us -> 133 us
    pallas_call x1, Pallas kernels: 64.8 us -> 62.7 us  [input_gradient(): pl.pallas_call(gradient_kernel, name='input_gradient', out_shape=jax.Shap...]
where the time goes in v5:
time: 135 us
  Pallas kernels  133 us (99%)
  local copies, waits for them, and re-layouts  1.78 us (1%)
    pallas_call x1, Pallas kernels, input_gradient(): pl.pallas_call(gradient_kernel, name='input_gradient', out_shape=jax.Shap...  62.7 us
    pallas_call x1, Pallas kernels, project_and_gather(): pl.pallas_call(project_kernel, name='project_and_gather', out_shape=(jax....  59.6 us
    pallas_call x1, Pallas kernels, attend(): pl.pallas_call(attend_kernel, name='attend', out_shape=(jax.ShapeDtypeStr...  10.4 us

profile of v5, /device:TPU:97, one launch (start us, length us, event | category | flops | bytes accessed | tf_op | source)
XLA Modules:
  0.0 134.5 jit_solution(15659700926783653433)
XLA Ops:
  0.0 59.6 %project_and_gather.1 = (bf16[4,128,128]{2,1,0:T(8,128)(2,1)}, bf16[4,4,2,128,256]{4,3,2,1,0:T(8,128)(2,1)}, bf16[4,128,128]{2,1,0:T(8,128)(2,1)}, bf16[4,1792,384]{2,1,0:T(8,128)(2,1)}) custom-call(bf16[256,7168]{1,0:T(8,128)(2,1)} %inp.1, bf16[3,448,256]{2,1,0:T(8,128)(2,1)} %bitcast.7, bf16[256,256]{1,0:T(8,128)(2,1)} %d_attn.1), custom_call_target="tpu_custom_call" | custom-call | tf_op jit(solution)/shard_map/project_and_gather/pallas_call | solution.py:374
  59.6 10.4 %attend.1 = (bf16[4,128,128]{2,1,0:T(8,128)(2,1)}, bf16[8,512,256]{2,1,0:T(8,128)(2,1)}) custom-call(s32[4,8]{1,0:T(4,128)} %bitcast.9, bf16[4,128,128]{2,1,0:T(8,128)(2,1)} %get-tuple-element.11.q_ref, bf16[8,512,256]{2,1,0:T(8,128)(2,1)} %bitcast.5, bf16[4,128,128]{2,1,0:T(8,128)(2,1)} %get-tuple-element.13.do_ref), custom_call_target="tpu_custom_call" | custom-call | tf_op jit(solution)/shard_map/attend/pallas_call | solution.py:460
  70.0 62.7 %input_gradient.1 = bf16[256,448]{1,0:T(8,128)(2,1)} custom-call(bf16[4,4,2,128,256]{4,3,2,1,0:T(8,128)(2,1)} %bitcast.6, bf16[512,128]{1,0:T(8,128)(2,1)} %bitcast.8, bf16[4,1792,384]{2,1,0:T(8,128)(2,1)} %get-tuple-element.16.w_in), custom_call_target="tpu_custom_call" | custom-call | tf_op jit(solution)/shard_map/input_gradient/pallas_call | solution.py:694
  132.8 1.8 %copy.5 = bf16[256,448]{0,1:T(8,128)(2,1)} copy(bf16[256,448]{1,0:T(8,128)(2,1)} %input_gradient.1) | data formatting | bytes 458752 | tf_op jit(solution)/shard_map/input_gradient/pallas_call | solution.py:694

commit v6 on v5

--- a/solution.py
+++ b/solution.py
@@ -400,9 +400,10 @@
     )(inputs, w3, d_attn)
 
 
-def attend_kernel(selected, q_ref, kv_ref, do_ref, dq_ref, dkv_ref, score, soft, total):
+def attend_kernel(selected, q_ref, kv_ref, do_ref, dq_ref, dkv_ref, score, dprob, pair, total):
     _, y, _, _, j = place()
     total[...] = jnp.zeros_like(total)
+    pair[...] = jnp.zeros_like(pair)
     contract = lambda a, b: (((a,), (b,)), ((), ()))
     dot = functools.partial(lax.dot_general, preferred_element_type=F32)
     key_at = lax.broadcasted_iota(jnp.int32, (BLOCK, HD), 0)
@@ -411,40 +412,36 @@
     def tile(run, carry):
         first = (run * 4 + y) * 256 + HD * j
         block = lax.div(first, BLOCK)
-        q = q_ref[run]
-        do = do_ref[run]
+        pair[:HD, :HD] = q_ref[run]
+        pair[HD:, HD:] = do_ref[run]
+        both = pair[...]
         highest = jnp.full((1, HD), -jnp.inf, F32)
         for t in range(TOP):
             chosen = selected[t, block]
             kb = jnp.maximum(chosen, 0)
-            s = dot(kv_ref[kb, :, :HD], q, contract(1, 1)) * SCALE
+            products = dot(kv_ref[kb], both, contract(1, 1))
             limit = jnp.where(chosen >= 0, first - kb * BLOCK, -2 * BLOCK)
-            s = jnp.where(key_at - query_at <= limit, s, -jnp.inf)
+            s = jnp.where(key_at - query_at <= limit, products[:, :HD] * SCALE, -jnp.inf)
             score[t] = s
+            dprob[t] = products[:, HD:]
             highest = jnp.maximum(highest, jnp.max(s, axis=0, keepdims=True))
         totals = jnp.zeros((1, HD), F32)
+        delta = jnp.zeros((1, HD), F32)
         for t in range(TOP):
             e = jnp.exp(score[t] - highest)
             score[t] = e
             totals += jnp.sum(e, axis=0, keepdims=True)
+            delta += jnp.sum(e * dprob[t], axis=0, keepdims=True)
         share = 1.0 / totals
-        attended = jnp.zeros((HD, HD), F32)
+        delta = delta * share
+        dq = jnp.zeros((HD, HD), F32)
         for t in range(TOP):
             kb = jnp.maximum(selected[t, block], 0)
             p = score[t] * share
-            low = p.astype(BF16)
-            score[t] = p
-            soft[t] = low
-            attended += dot(kv_ref[kb, :, HD:], low, contract(0, 0))
-        attended = attended.astype(BF16).astype(F32)
-        delta = jnp.sum(do.astype(F32).T * attended, axis=0, keepdims=True)
-        dq = jnp.zeros((HD, HD), F32)
-        for t in range(TOP):
-            kb = jnp.maximum(selected[t, block], 0)
-            dp = dot(kv_ref[kb, :, HD:], do, contract(1, 1))
-            ds = (score[t] * (dp - delta)).astype(BF16)
-            total[kb, :, :HD] += dot(ds, q, contract(1, 0))
-            total[kb, :, HD:] += dot(soft[t], do, contract(1, 0))
+            ds = (p * (dprob[t] - delta)).astype(BF16)
+            total[kb] += dot(
+                jnp.concatenate([ds, p.astype(BF16)], axis=1), both, contract(1, 0)
+            )
             dq += dot(ds, kv_ref[kb, :, :HD], contract(0, 0))
         dq_ref[run] = (dq * SCALE).astype(BF16)
         return carry
@@ -468,7 +465,8 @@
         out_specs=(vmem, vmem),
         scratch_shapes=[
             pltpu.VMEM((TOP, BLOCK, HD), F32),
-            pltpu.VMEM((TOP, BLOCK, HD), BF16),
+            pltpu.VMEM((TOP, BLOCK, HD), F32),
+            pltpu.VMEM((2 * HD, 2 * HD), BF16),
             pltpu.VMEM((8, BLOCK, 2 * HD), F32),
         ],
         compiler_params=pltpu.CompilerParams(vmem_limit_bytes=VMEM_BYTES),

time: 135 us -> 134 us (level)
  no operation moved by 1% of the time
where the time goes in v6:
time: 134 us
  Pallas kernels  132 us (99%)
  local copies, waits for them, and re-layouts  1.78 us (1%)
    pallas_call x1, Pallas kernels, input_gradient(): pl.pallas_call(gradient_kernel, name='input_gradient', out_shape=jax.Shap...  62.7 us
    pallas_call x1, Pallas kernels, project_and_gather(): pl.pallas_call(project_kernel, name='project_and_gather', out_shape=(jax....  59.6 us
    pallas_call x1, Pallas kernels, attend(): pl.pallas_call(attend_kernel, name='attend', out_shape=(jax.ShapeDtypeStr...  9.54 us

profile of v6, /device:TPU:97, one launch (start us, length us, event | category | flops | bytes accessed | tf_op | source)
XLA Modules:
  0.0 133.7 jit_solution(5332986082985071871)
XLA Ops:
  0.0 59.6 %project_and_gather.1 = (bf16[4,128,128]{2,1,0:T(8,128)(2,1)}, bf16[4,4,2,128,256]{4,3,2,1,0:T(8,128)(2,1)}, bf16[4,128,128]{2,1,0:T(8,128)(2,1)}, bf16[4,1792,384]{2,1,0:T(8,128)(2,1)}) custom-call(bf16[256,7168]{1,0:T(8,128)(2,1)} %inp.1, bf16[3,448,256]{2,1,0:T(8,128)(2,1)} %bitcast.7, bf16[256,256]{1,0:T(8,128)(2,1)} %d_attn.1), custom_call_target="tpu_custom_call" | custom-call | tf_op jit(solution)/shard_map/project_and_gather/pallas_call | solution.py:374
  59.6 9.5 %attend.1 = (bf16[4,128,128]{2,1,0:T(8,128)(2,1)}, bf16[8,512,256]{2,1,0:T(8,128)(2,1)}) custom-call(s32[4,8]{1,0:T(4,128)} %bitcast.9, bf16[4,128,128]{2,1,0:T(8,128)(2,1)} %get-tuple-element.11.q_ref, bf16[8,512,256]{2,1,0:T(8,128)(2,1)} %bitcast.5, bf16[4,128,128]{2,1,0:T(8,128)(2,1)} %get-tuple-element.13.do_ref), custom_call_target="tpu_custom_call" | custom-call | tf_op jit(solution)/shard_map/attend/pallas_call | solution.py:457
  69.2 62.7 %input_gradient.1 = bf16[256,448]{1,0:T(8,128)(2,1)} custom-call(bf16[4,4,2,128,256]{4,3,2,1,0:T(8,128)(2,1)} %bitcast.6, bf16[512,128]{1,0:T(8,128)(2,1)} %bitcast.8, bf16[4,1792,384]{2,1,0:T(8,128)(2,1)} %get-tuple-element.16.w_in), custom_call_target="tpu_custom_call" | custom-call | tf_op jit(solution)/shard_map/input_gradient/pallas_call | solution.py:692
  131.9 1.8 %copy.5 = bf16[256,448]{0,1:T(8,128)(2,1)} copy(bf16[256,448]{1,0:T(8,128)(2,1)} %input_gradient.1) | data formatting | bytes 458752 | tf_op jit(solution)/shard_map/input_gradient/pallas_call | solution.py:692

commit v7 on v6

--- a/solution.py
+++ b/solution.py
@@ -674,10 +674,9 @@
     for h in (0, 1):
         for k in (0, 1):
             got(fin_in.at[h, k], f_sems.at[h, k])
-    for k in (0, 1):
-        out[pl.ds(HD * k, HD)] = (
-            (fin_in[0, k].astype(F32) + fin_in[1, k].astype(F32)).T
-        ).astype(BF16)
+    for h in (0, 1):
+        for k in (0, 1):
+            out[h, pl.ds(HD * k, HD)] = fin_in[h, k].T
     mail.flush()
 
 
@@ -692,7 +691,7 @@
     return pl.pallas_call(
         gradient_kernel,
         name="input_gradient",
-        out_shape=jax.ShapeDtypeStruct((2 * HD, d), BF16),
+        out_shape=jax.ShapeDtypeStruct((2, 2 * HD, d), BF16),
         in_specs=[vmem, vmem, any_space],
         out_specs=vmem,
         scratch_shapes=[
@@ -725,7 +724,8 @@
     dq, dkv = attend(
         selected.T, q, kv.reshape(8, BLOCK, 2 * HD), do
     )
-    return input_gradient(dkv.reshape(4, 4, 2, HD, 2 * HD), dq.reshape(4 * HD, HD), w_all)
+    halves = input_gradient(dkv.reshape(4, 4, 2, HD, 2 * HD), dq.reshape(4 * HD, HD), w_all)
+    return (halves[0].astype(F32) + halves[1].astype(F32)).astype(BF16)
 
 
 def solution(mesh):

time: 134 us -> 134 us (level)
    pallas_call x1 -> x0, local copies, waits for them, and re-layouts: 1.78 us -> none  [input_gradient(): pl.pallas_call(gradient_kernel, name='input_gradient', out_shape=jax.Shap...]
where the time goes in v7:
time: 134 us
  Pallas kernels  132 us (99%)
    pallas_call x1, Pallas kernels, input_gradient(): pl.pallas_call(gradient_kernel, name='input_gradient', out_shape=jax.Shap...  62.9 us
    pallas_call x1, Pallas kernels, project_and_gather(): pl.pallas_call(project_kernel, name='project_and_gather', out_shape=(jax....  59.6 us
    pallas_call x1, Pallas kernels, attend(): pl.pallas_call(attend_kernel, name='attend', out_shape=(jax.ShapeDtypeStr...  9.54 us

profile of v7, /device:TPU:97, one launch (start us, length us, event | category | flops | bytes accessed | tf_op | source)
XLA Modules:
  0.0 134.0 jit_solution(207694900773957809)
XLA Ops:
  0.0 59.6 %project_and_gather.1 = (bf16[4,128,128]{2,1,0:T(8,128)(2,1)}, bf16[4,4,2,128,256]{4,3,2,1,0:T(8,128)(2,1)}, bf16[4,128,128]{2,1,0:T(8,128)(2,1)}, bf16[4,1792,384]{2,1,0:T(8,128)(2,1)}) custom-call(bf16[256,7168]{1,0:T(8,128)(2,1)} %inp.1, bf16[3,448,256]{2,1,0:T(8,128)(2,1)} %bitcast.9, bf16[256,256]{1,0:T(8,128)(2,1)} %d_attn.1), custom_call_target="tpu_custom_call" | custom-call | tf_op jit(solution)/shard_map/project_and_gather/pallas_call | solution.py:374
  59.6 9.5 %attend.1 = (bf16[4,128,128]{2,1,0:T(8,128)(2,1)}, bf16[8,512,256]{2,1,0:T(8,128)(2,1)}) custom-call(s32[4,8]{1,0:T(4,128)} %bitcast.11, bf16[4,128,128]{2,1,0:T(8,128)(2,1)} %get-tuple-element.11.q_ref, bf16[8,512,256]{2,1,0:T(8,128)(2,1)} %bitcast.7, bf16[4,128,128]{2,1,0:T(8,128)(2,1)} %get-tuple-element.13.do_ref), custom_call_target="tpu_custom_call" | custom-call | tf_op jit(solution)/shard_map/attend/pallas_call | solution.py:457
  69.2 62.9 %input_gradient.1 = bf16[2,256,448]{2,1,0:T(8,128)(2,1)} custom-call(bf16[4,4,2,128,256]{4,3,2,1,0:T(8,128)(2,1)} %bitcast.8, bf16[512,128]{1,0:T(8,128)(2,1)} %bitcast.10, bf16[4,1792,384]{2,1,0:T(8,128)(2,1)} %get-tuple-element.16.w_in), custom_call_target="tpu_custom_call" | custom-call | tf_op jit(solution)/shard_map/input_gradient/pallas_call | solution.py:691
  132.0 1.1 fusion
  133.1 0.8 copy.5
